TPU v7x, 512 devices: a whole 4x8x8 slice. The times are simulated.
512 devices in a mesh: seq: 32 (over z, y_hi), doc: 16 (over x, y_lo, core).
Axes of the slice: x: 4, y: 8 (y_hi: 4, y_lo: 2; y = y_hi * 2 + y_lo), z: 8, core: 2. Of those that a mesh axis runs over, the one named last changes fastest.
Arguments:
- byte_q: bfloat16 [262144, 1024], P(('doc', 'seq')), parts along dimension 0, may hold values from -6 to 6
- byte_k: bfloat16 [262144, 1024], P(('doc', 'seq')), parts along dimension 0, may hold values from -6 to 6
- byte_v: bfloat16 [262144, 1024], P(('doc', 'seq')), parts along dimension 0, may hold values from -6 to 6
- byte_gain: bfloat16 [1024], replicated, may hold values from 0.2 to 4.5
- pool_query: bfloat16 [8, 128], replicated, may hold values from -12 to 12
- w_up: bfloat16 [1024, 2048], P('seq'), may hold values from -1 to 1
- patch_gain: bfloat16 [2048], replicated, may hold values from 0.099609375 to 1.8984375
- w_kv: bfloat16 [2048, 1024], P('seq'), may hold values from -1 to 1
- out_gain: bfloat16 [2048], replicated, may hold values from 0.2 to 4.5
- dec_gain: bfloat16 [1024], replicated, may hold values from 0.099609375 to 1.8984375
- patch_start: int32 [512, 80], P('doc'), parts along dimension 0, may hold values from 0 to 512, as said below
Outputs:
- byte_out: bfloat16 [262144, 1024], P(('doc', 'seq')), parts along dimension 0
- patch_out: bfloat16 [40960, 2048], P(('doc', 'seq')), parts along dimension 0
There are 16 independent parts, one for each index of `doc`. A program takes and returns all parts, laid end to end along the dimension named above; an argument that names none is the same for every part. Nothing has to cross between parts.
Inputs may be any that keep to these rules, and one draw needn't show every extreme that they name: `patch_start`: row r lists the patch starts of block r: 0 first, strictly rising over its live slots, then 512 in every unused slot; each row has at least 20 live slots, and some row has all 80 live.
All inputs are finite; a program needn't handle non-finite values.
Results may differ from a plain program's by a relative error of at most 0.0085.
Values may be sent and summed in bfloat16 or wider, within the bound.
A program may use at most 128 MiB of HBM per device.

v0:
```python
import jax
import jax.numpy as jnp
from jax import lax
from jax.sharding import PartitionSpec as P

HB = 8
HD = 128
PATCH_QUERY_HEADS = 32
PATCH_KEY_HEADS = 8
PATCH_HEAD_SIZE = 64
PATCH_SLOTS = 80


epsilon = 1e-06


def joined_along(blocks, dim):
    dims = list(blocks.shape[1:])
    dims[dim] *= blocks.shape[0]
    return jnp.moveaxis(blocks, 0, dim).reshape(dims)


def gather_together(arrays, axis, dims):
    ravelled = jnp.concatenate([a.reshape(-1) for a in arrays])
    lines, at, finished = (lax.all_gather(ravelled, axis), 0, [])
    for a, dim in zip(arrays, dims):
        blocks = lines[:, at : at + a.size].reshape(-1, *a.shape)
        finished.append(joined_along(blocks, dim))
        at += a.size
    return tuple(finished)


def passed_along(value, axis, steps):
    count = lax.axis_size(axis)
    first, last = (max(0, -steps), min(count, count - steps))
    return lax.ppermute(value, axis, [(source, source + steps) for source in range(first, last)])


def normed(matrix, gains):
    return (
        matrix
        * lax.rsqrt(jnp.mean(matrix * matrix, axis=-1, keepdims=True) + epsilon)
        * gains.astype(jnp.float32)
    )


def masked_weights(scores, allowed):
    scores = jnp.where(allowed, scores, -jnp.inf)
    peak = jnp.max(scores, axis=-1, keepdims=True)
    expo = jnp.where(allowed, jnp.exp(scores - peak), 0.0)
    return (expo / jnp.sum(expo, axis=-1, keepdims=True)).astype(jnp.bfloat16)


def byte_attention(query_rows, key_rows, value_rows, leading):
    nbytes = query_rows.shape[0]
    reach = key_rows.shape[0] - nbytes
    query_head_rows = query_rows.reshape(nbytes, HB, HD).transpose(1, 0, 2)
    key_head_rows = key_rows.reshape(nbytes + reach, HB, HD).transpose(1, 0, 2)
    value_head_rows = value_rows.reshape(nbytes + reach, HB, HD).transpose(1, 0, 2)
    row_pos = jnp.arange(nbytes, dtype=jnp.int32)[:, None]
    col_pos = jnp.arange(nbytes + reach, dtype=jnp.int32)[None, :]
    allowed = (
        (col_pos > row_pos)
        & (col_pos <= row_pos + reach)
        & ((col_pos >= reach) | jnp.logical_not(leading))
    )

    def one_head(operands):
        head_query, head_key, head_value = operands
        scores = jnp.dot(head_query, head_key.T, preferred_element_type=jnp.float32) * HD ** (-0.5)
        weights = masked_weights(scores, allowed)
        return jnp.dot(weights, head_value, preferred_element_type=jnp.float32)

    mixed = lax.map(one_head, (query_head_rows, key_head_rows, value_head_rows))
    return mixed.transpose(1, 0, 2).reshape(nbytes, HB * HD)


def segments(starts, nbytes):
    positions = jnp.arange(nbytes, dtype=jnp.int32)
    segment = jnp.sum((starts[None, :] <= positions[:, None]).astype(jnp.int32), axis=1) - 1
    member = segment[None, :] == jnp.arange(starts.shape[0], dtype=jnp.int32)[:, None]
    return (segment, member)


def pool(encoded, member, pool_query):
    nbytes = encoded.shape[0]
    enc_heads = encoded.reshape(nbytes, HB, HD)
    scores = jnp.einsum(
        "bhd,hd->bh", enc_heads, pool_query, preferred_element_type=jnp.float32
    ) * HD ** (-0.5)
    inside = member[:, :, None]
    highest = jnp.max(jnp.where(inside, scores[None], -jnp.inf), axis=1)
    own_max = jnp.max(jnp.where(inside, highest[:, None, :], -jnp.inf), axis=0)
    expo = jnp.exp(scores - own_max)
    totals = jnp.sum(jnp.where(inside, expo[None], 0.0), axis=1)
    divisor = jnp.max(jnp.where(inside, totals[:, None, :], 0.0), axis=0)
    weights = (expo / divisor).astype(jnp.bfloat16)
    spread = jnp.where(inside, weights[None], jnp.zeros((), jnp.bfloat16))
    pooled = jnp.einsum("pbh,bhd->phd", spread, enc_heads, preferred_element_type=jnp.float32)
    return pooled.reshape(member.shape[0], HB * HD).astype(jnp.bfloat16)


def decode(encoded, patch_rows, segment):
    nbytes = encoded.shape[0]
    slot_total_count = patch_rows.shape[0]
    enc_heads = encoded.reshape(nbytes, HB, HD)
    packed = patch_rows.reshape(slot_total_count, HB, 2, HD)
    scores = jnp.einsum(
        "bhd,phd->hbp", enc_heads, packed[:, :, 0], preferred_element_type=jnp.float32
    ) * HD ** (-0.5)
    allowed = jnp.arange(slot_total_count, dtype=jnp.int32)[None, :] <= segment[:, None]
    weights = masked_weights(scores, allowed[None])
    mixed = jnp.einsum("hbp,phd->bhd", weights, packed[:, :, 1], preferred_element_type=jnp.float32)
    return mixed.reshape(nbytes, HB * HD)


def per_device(
    byte_q,
    byte_k,
    byte_v,
    byte_gain,
    pool_query,
    w_up,
    patch_gain,
    w_kv,
    out_gain,
    dec_gain,
    patch_start,
):
    nbytes = byte_q.shape[0]
    device = lax.axis_index("seq")
    head_groups = PATCH_QUERY_HEADS // PATCH_KEY_HEADS
    up_whole, kv_whole = gather_together((w_up, w_kv), "seq", (0, 0))
    tails = passed_along((byte_k, byte_v), "seq", 1)
    key_rows = jnp.concatenate([tails[0], byte_k], axis=0)
    value_rows = jnp.concatenate([tails[1], byte_v], axis=0)
    encoded = normed(byte_attention(byte_q, key_rows, value_rows, device == 0), byte_gain).astype(
        jnp.bfloat16
    )
    starts = lax.dynamic_index_in_dim(patch_start, device, 0, keepdims=False)
    segment, member = segments(starts, nbytes)
    pooled = pool(encoded, member, pool_query)
    lifted = jnp.dot(pooled, up_whole, preferred_element_type=jnp.float32)
    patch_input = normed(lifted, patch_gain).astype(jnp.bfloat16)
    key_value_pairs = jnp.dot(patch_input, kv_whole, preferred_element_type=jnp.float32).astype(
        jnp.bfloat16
    )
    counts = jnp.sum((patch_start < nbytes).astype(jnp.int32), axis=1)
    live_grid = jnp.arange(PATCH_SLOTS, dtype=jnp.int32)[None, :] < counts[:, None]
    is_live = live_grid.reshape(-1)
    query_start = device * PATCH_SLOTS
    query_pos = query_start + jnp.arange(PATCH_SLOTS, dtype=jnp.int32)
    query_head_rows = patch_input.reshape(
        PATCH_SLOTS, PATCH_KEY_HEADS, head_groups, PATCH_HEAD_SIZE
    ).transpose(1, 2, 0, 3)
    start_state = (
        jnp.full((PATCH_KEY_HEADS, head_groups, PATCH_SLOTS), -1e30, jnp.float32),
        jnp.zeros((PATCH_KEY_HEADS, head_groups, PATCH_SLOTS), jnp.float32),
        jnp.zeros((PATCH_KEY_HEADS, head_groups, PATCH_SLOTS, PATCH_HEAD_SIZE), jnp.float32),
    )
    block_rows = lax.all_gather(key_value_pairs, "seq", axis=0, tiled=True)
    row_count = block_rows.shape[0]

    def compute():
        peak_old, norm_sum, summed = start_state
        key_head_rows = block_rows[:, : PATCH_KEY_HEADS * PATCH_HEAD_SIZE].reshape(
            row_count, PATCH_KEY_HEADS, PATCH_HEAD_SIZE
        )
        value_head_rows = block_rows[:, PATCH_KEY_HEADS * PATCH_HEAD_SIZE :].reshape(
            row_count, PATCH_KEY_HEADS, PATCH_HEAD_SIZE
        )
        key_pos = jnp.arange(row_count, dtype=jnp.int32)
        allowed = (key_pos[None, :] <= query_pos[:, None]) & is_live[None, :]
        scores = jnp.einsum(
            "kgqd,pkd->kgqp", query_head_rows, key_head_rows, preferred_element_type=jnp.float32
        ) * PATCH_HEAD_SIZE ** (-0.5)
        scores = jnp.where(allowed, scores, -1e30)
        peak_new = jnp.maximum(peak_old, jnp.max(scores, axis=-1))
        expo = jnp.where(allowed, jnp.exp(scores - peak_new[..., None]), 0.0)
        norm_sum = jnp.sum(expo, axis=-1)
        summed = jnp.einsum(
            "kgqp,pkd->kgqd",
            expo.astype(jnp.bfloat16),
            value_head_rows,
            preferred_element_type=jnp.float32,
        )
        return (peak_new, norm_sum, summed)

    peak_end, norm_sum, summed = lax.cond(
        jnp.int32(0) <= query_start + PATCH_SLOTS - 1, compute, lambda: start_state
    )
    mixed = summed / norm_sum[..., None]
    mixed = mixed.transpose(2, 0, 1, 3).reshape(PATCH_SLOTS, PATCH_QUERY_HEADS * PATCH_HEAD_SIZE)
    alive = lax.dynamic_index_in_dim(live_grid, device, 0, keepdims=False)
    patch_out = (normed(mixed, out_gain) * alive[:, None].astype(jnp.float32)).astype(jnp.bfloat16)
    byte_out = normed(decode(encoded, patch_out, segment), dec_gain).astype(jnp.bfloat16)
    return (byte_out, patch_out)


def solution(mesh):
    placed = (
        P(("doc", "seq"), None),
        P(("doc", "seq"), None),
        P(("doc", "seq"), None),
        P(),
        P(),
        P("seq", None),
        P(),
        P("seq", None),
        P(),
        P(),
        P("doc", None),
    )
    return jax.shard_map(
        per_device,
        mesh=mesh,
        in_specs=placed,
        out_specs=(P(("doc", "seq"), None), P(("doc", "seq"), None)),
        check_vma=False,
    )
```

profile of v0, /device:TPU:10, one launch (start us, length us, event | category | flops | bytes accessed | tf_op | source)
XLA Modules:
  0.0 405.7 jit_solution(14062340675311319840)
XLA Ops:
  7.2 1.0 copy.70
  10.0 2.3 copy.50
  12.3 5.6 %collective-permute-start.1 = (bf16[512,1024]{0,1:T(8,128)(2,1)}, bf16[512,1024]{0,1:T(8,128)(2,1)}, u32[]{:S(2)}, u32[]{:S(2)}) collective-permute-start(bf16[512,1024]{0,1:T(8,128)(2,1)} %copy.50), channel_id=1, source_target_pairs={{0,16},{16,32},{32,48},{48,64},{64,80},{80,96},{96,112},{112,128},... | collective-permute-start | bytes 3145736 | tf_op jit(solution)/shard_map/ppermute | solution.py:36
  18.4 4.9 %collective-permute-start = (bf16[512,1024]{0,1:T(8,128)(2,1)S(1)}, bf16[512,1024]{0,1:T(8,128)(2,1)}, u32[]{:S(2)}, u32[]{:S(2)}) collective-permute-start(bf16[512,1024]{0,1:T(8,128)(2,1)S(1)} %copy.48), channel_id=1, source_target_pairs={{0,16},{16,32},{32,48},{48,64},{64,80},{80,96},{96,112},{112,128},... | collective-permute-start | bytes 3145736 | tf_op jit(solution)/shard_map/ppermute | solution.py:36
  23.3 2.3 copy.47
  25.8 52.9 %collective-permute-done.1 = bf16[512,1024]{0,1:T(8,128)(2,1)} collective-permute-done((bf16[512,1024]{0,1:T(8,128)(2,1)}, bf16[512,1024]{0,1:T(8,128)(2,1)}, u32[]{:S(2)}, u32[]{:S(2)}) %collective-permute-start.1) | collective-permute-done | bytes 1048608 | tf_op jit(solution)/shard_map/ppermute | solution.py:36
  78.7 3.2 pad_maximum_fusion.1
  81.9 44.5 %collective-permute-done = bf16[512,1024]{0,1:T(8,128)(2,1)} collective-permute-done((bf16[512,1024]{0,1:T(8,128)(2,1)S(1)}, bf16[512,1024]{0,1:T(8,128)(2,1)}, u32[]{:S(2)}, u32[]{:S(2)}) %collective-permute-start) | collective-permute-done | bytes 1048608 | tf_op jit(solution)/shard_map/ppermute | solution.py:36
  126.5 2.8 pad_maximum_fusion
  129.3 37.3 %while.11 = (s32[]{:T(128)}, f32[8,512,128]{2,1,0:T(8,128)S(1)}, bf16[8,512,128]{1,2,0:T(8,128)(2,1)}, bf16[8,1024,128]{1,2,0:T(8,128)(2,1)}, bf16[8,1024,128]{1...) while((s32[]{:T(128)}, f32[8,512,128]{2,1,0:T(8,128)S(1)}, ...), condition=%wide.region_3.4_spmd.clone, body=%wide.region_0.3_spmd.clone.sunk | while | flops 282065920 | bytes 7230549 | solution.py:74
  129.3 1.8 fusion.96
  131.1 0.9 fusion.97
  132.1 1.9 fusion.98
  134.0 1.8 fusion.96
  135.8 0.9 fusion.97
  136.7 1.9 fusion.98
  138.7 1.8 fusion.96
  141.4 1.9 fusion.98
  143.3 1.8 fusion.96
  146.1 1.9 fusion.98
  148.0 1.8 fusion.96
  149.8 0.9 fusion.97
  150.7 1.9 fusion.98
  152.7 1.8 fusion.96
  155.4 1.9 fusion.98
  157.4 1.8 fusion.96
  159.1 0.9 fusion.97
  160.1 1.9 fusion.98
  162.0 1.8 fusion.96
  164.7 1.9 fusion.98
  168.5 31.3 %all-gather.6.cloned.1.call-done = bf16[4194304]{0:T(1024)(128)(2,1)} async-done(((bf16[131072]{0:T(1024)(128)(2,1)}), bf16[4194304]{0:T(1024)(128)(2,1)}) %all-gather.6.cloned.1.call-update) | async-done | bytes 8388624 | tf_op jit(solution)/shard_map/all_gather | solution.py:25
  199.8 8.7 %reshape.198 = bf16[32,131072]{1,0:T(8,128)(2,1)} reshape(bf16[4194304]{0:T(1024)(128)(2,1)} %all-gather.6.cloned.1.call-done) | data formatting | bytes 16777216 | tf_op jit(solution)/shard_map/all_gather | solution.py:25
  208.5 5.7 %fusion.76 = (bf16[32,65536]{1,0:T(8,128)(2,1)}, bf16[32,65536]{1,0:T(8,128)(2,1)}) fusion(bf16[32,131072]{1,0:T(8,128)(2,1)} %reshape.198), kind=kLoop, calls=%fused_computation.124 | loop fusion | bytes 16777216 | tf_op jit(solution)/shard_map/slice | solution.py:27
  214.2 5.6 %reshape_reshape.6 = bf16[1024,2048]{1,0:T(8,128)(2,1)} reshape(bf16[32,65536]{1,0:T(8,128)(2,1)} %get-tuple-element.144) | data formatting | bytes 8388608 | tf_op jit(solution)/shard_map/reshape;reshape | solution.py:20
  219.8 3.2 multiply_reduce_fusion.1
  223.0 5.6 %reshape_reshape.7 = bf16[2048,1024]{1,0:T(8,128)(2,1)} reshape(bf16[32,65536]{1,0:T(8,128)(2,1)} %get-tuple-element.143) | data formatting | bytes 8388608 | tf_op jit(solution)/shard_map/reshape;reshape | solution.py:20
  228.8 3.7 convolution_convert_fusion
  233.1 111.2 %all-gather.4.cloned.1.call-done = bf16[2560,1024]{1,0:T(8,128)(2,1)} async-done(((bf16[80,1024]{1,0:T(8,128)(2,1)}), bf16[2560,1024]{1,0:T(8,128)(2,1)}) %all-gather.4.cloned.1.call-update) | async-done | bytes 5242896 | tf_op jit(solution)/shard_map/all_gather | solution.py:161
  344.4 44.2 %conditional.1 = (f32[8,4,80]{2,1,0:T(4,128)S(1)}, f32[8,4,80,64]{2,3,1,0:T(8,128)S(1)}) conditional(s32[]{:T(128)} %convert_element_type.73, () %tuple.20, (s32[]{:T(128)}, s32[80]{0:T(128)S(1)}, pred[32,80]{1,0:T(8,128)(4,1)S(1)}, bf16[2560,1024]{1,0:T(8,128)(2,1)}, bf16[8,4,80,64]{2,3,1,0:T(8,128)(2,1)S(1)}) %tuple.63), branch_computations={%region_12.13_spmd, %region_13.16_spmd} | conditional | flops 1763325440 | bytes 106729936 | solution.py:189
  344.7 7.8 %copy.57 = bf16[2560,1024]{0,1:T(8,128)(2,1)} copy(bf16[2560,1024]{1,0:T(8,128)(2,1)} %get-tuple-element.117) | data formatting | bytes 10485760 | tf_op jit(solution)/shard_map
  352.4 2.9 fusion.75
  355.3 11.0 %fusion.2 = (f32[8,4,80]{2,1,0:T(4,128)S(1)}, f32[8,4,80,2560]{3,2,1,0:T(8,128)}) fusion(pred[80,2560]{1,0:T(8,128)(4,1)S(1)} %fusion.8, bf16[8,4,80,64]{2,3,1,0:T(8,128)(2,1)S(1)} %get-tuple-element.46, bf16[2560,8,64,1]{0,2,3,1:T(8,128)(2,1)S(1)} %bitcast.128), kind=kOutput, calls=%fused_computation.3 | convolution fusion | flops 858519040 | bytes 29378560 | tf_op jit(solution)/shard_map/cond/branch_1_fun/kgqd,pkd->kgqp/dot_general | solution.py:174
  366.3 11.9 %fusion.5 = f32[8,4,80,64]{2,3,1,0:T(8,128)S(1)} fusion(bf16[2560,8,64,1]{0,2,3,1:T(8,128)(2,1)S(1)} %bitcast.130, f32[8,4,80,2560]{3,2,1,0:T(8,128)} %get-tuple-element.140, f32[8,4,80]{2,1,0:T(4,128)S(1)} %broadcast_maximum_fusion, pred[80,2560]{1,0:T(8,128)(4,1)S(1)} %fusion.8), kind=kOutput, calls=%fused_computation.6 | convolution fusion | flops 871628800 | bytes 29706240 | tf_op jit(solution)/shard_map/cond/branch_1_fun/kgqp,pkd->kgqd/dot_general | solution.py:181
  378.3 10.3 %fusion.4 = f32[8,4,80]{2,1,0:T(4,128)S(1)} fusion(f32[8,4,80,2560]{3,2,1,0:T(8,128)} %get-tuple-element.140, f32[8,4,80]{2,1,0:T(4,128)S(1)} %broadcast_maximum_fusion, pred[80,2560]{1,0:T(8,128)(4,1)S(1)} %fusion.8), kind=kLoop, calls=%fused_computation.5 | loop fusion | flops 32765440 | bytes 26439680 | tf_op jit(solution)/shard_map/cond/branch_1_fun/reduce_sum | solution.py:180
  391.0 1.7 fusion.79
  393.7 2.0 fusion.33
  395.7 1.9 copy.60
  397.7 1.2 multiply_convert_fusion
  (73 shorter events, 12.3 us)
Async XLA Ops:
  7.2 160.1 %copy-start = (bf16[8,128]{1,0:T(8,128)(2,1)S(1)}, bf16[8,128]{1,0:T(8,128)(2,1)}, u32[]{:S(2)}) copy-start(bf16[8,128]{1,0:T(8,128)(2,1)} %param.19) | copy-start | bytes 6148
  7.2 10.7 %copy-start.2 = (bf16[512,1024]{1,0:T(8,128)(2,1)S(1)}, bf16[512,1024]{1,0:T(8,128)(2,1)}, u32[]{:S(2)}) copy-start(bf16[512,1024]{1,0:T(8,128)(2,1)} %param.16) | copy-start | bytes 3145732
  7.2 192.6 %all-gather.6.cloned.1.call-start = ((), (), s32[]{:S(2)}) async-start(), calls=%async_computation.1 | async-start | bytes 8650752 | tf_op jit(solution)/shard_map/all_gather | solution.py:25
  9.9 334.4 %all-gather.4.cloned.1.call-start = ((), (), s32[]{:S(2)}) async-start(), calls=%async_computation | async-start | bytes 5406720 | tf_op jit(solution)/shard_map/all_gather | solution.py:161
  12.3 13.4 %copy-start.6 = (bf16[2048]{0:T(1024)(128)(2,1)S(1)}, bf16[2048]{0:T(1024)(128)(2,1)}, u32[]{:S(2)}) copy-start(bf16[2048]{0:T(1024)(128)(2,1)} %param.21) | copy-start | bytes 12292
  12.3 13.4 %copy-start.5 = (s32[32,80]{1,0:T(8,128)S(1)}, s32[32,80]{1,0:T(8,128)}, u32[]{:S(2)}) copy-start(s32[32,80]{1,0:T(8,128)} %param.25) | copy-start | bytes 30724
  12.3 13.5 %copy-start.8 = (bf16[1024]{0:T(1024)(128)(2,1)S(1)}, bf16[1024]{0:T(1024)(128)(2,1)}, u32[]{:S(2)}) copy-start(bf16[1024]{0:T(1024)(128)(2,1)} %param.18) | copy-start | bytes 6148
  12.3 66.5 %collective-permute-start.1 = (bf16[512,1024]{0,1:T(8,128)(2,1)}, bf16[512,1024]{0,1:T(8,128)(2,1)}, u32[]{:S(2)}, u32[]{:S(2)}) collective-permute-start(bf16[512,1024]{0,1:T(8,128)(2,1)} %copy.50), channel_id=1, source_target_pairs={{0,16},{16,32},{32,48},{48,64},{64,80},{80,96},{96,112},{112,128},... | collective-permute-start | bytes 3145736 | tf_op jit(solution)/shard_map/ppermute | solution.py:36
  18.4 108.1 %collective-permute-start = (bf16[512,1024]{0,1:T(8,128)(2,1)S(1)}, bf16[512,1024]{0,1:T(8,128)(2,1)}, u32[]{:S(2)}, u32[]{:S(2)}) collective-permute-start(bf16[512,1024]{0,1:T(8,128)(2,1)S(1)} %copy.48), channel_id=1, source_target_pairs={{0,16},{16,32},{32,48},{48,64},{64,80},{80,96},{96,112},{112,128},... | collective-permute-start | bytes 3145736 | tf_op jit(solution)/shard_map/ppermute | solution.py:36
  228.8 3.8 copy-start.7
  228.8 3.8 copy-start.9
  389.8 0.7 copy-start.3
  391.0 2.7 copy-start.4
  395.7 3.2 copy-start.1
Sparse Core Ops, SparseCore 0:
  11.7 188.0 all-gather.5
  232.7 111.6 all-gather.3
where the time goes:
time: 407 us; the launch traced here: 406 us
  waiting for transfers between devices  240 us (59%)
  matrix products  64.4 us (16%)
  local copies, waits for them, and re-layouts  47.7 us (12%)
  other arithmetic  28.6 us (7%)
  between operations  14.3 us (4%)
  starting transfers between devices  10.6 us (3%)
    all_gather x1, waiting for transfers between devices, per_device(): block_rows = lax.all_gather(key_value_pairs, 'seq', axis=0, tiled=True)  111 us
    ppermute x2, waiting for transfers between devices, passed_along(): lax.ppermute(value, axis, [(source, source + steps) for source in range(f...  97.5 us
    all_gather x1, waiting for transfers between devices, gather_together(): lines, at, finished = (lax.all_gather(ravelled, axis), 0, [])  31.3 us
    dot_general x8, matrix products, one_head(): return jnp.dot(weights, head_value, preferred_element_type=jnp.float32)  15.4 us
    dot_general x8, matrix products, one_head(): jnp.dot(head_query, head_key.T, preferred_element_type=jnp.float32)  14.2 us
    dot_general x1, matrix products, compute(): jnp.einsum('kgqp,pkd->kgqd', expo.astype(jnp.bfloat16), value_head_rows,...  11.9 us
    another operation x2, local copies, waits for them, and re-layouts, joined_along(): return jnp.moveaxis(blocks, 0, dim).reshape(dims)  11.3 us
    dot_general x1, matrix products, compute(): jnp.einsum('kgqd,pkd->kgqp', query_head_rows, key_head_rows, preferred_el...  11 us
  transfers between devices with their start and end apart: 4, of which 4 were waited for; matrix products, arithmetic and copies ran while one was open for 13% of the time, Pallas kernels for 0%

commit v1 on v0

v1 whole, which is shorter than its diff:
```python
import functools

import jax
import jax.numpy as jnp
from jax import lax
from jax.experimental import pallas as pl
from jax.experimental.pallas import tpu as pltpu
from jax.sharding import PartitionSpec as P

EPS = 1e-06
LOG2E = 1.4426950408889634
BYTE_SCALE = 128 ** (-0.5) * LOG2E
PATCH_SCALE = 64 ** (-0.5) * LOG2E
NEG = -1e30
F32 = jnp.float32
BF16 = jnp.bfloat16
MESH = pl.DeviceIdType.MESH
NEAR_FIRST = (1, 7, 2, 6, 3, 5, 4)


def dot(a, b):
    return lax.dot_general(a, b, (((1,), (0,)), ((), ())), preferred_element_type=F32)


def dot_t(a, b):
    return lax.dot_general(a, b, (((1,), (1,)), ((), ())), preferred_element_type=F32)


def iota(shape, dim):
    return lax.broadcasted_iota(jnp.int32, shape, dim)


def as_row(column):
    return jnp.transpose(jnp.broadcast_to(column, (column.shape[0], 128)))[0:1]


def main_kernel(
    q_hbm, k_hbm, v_hbm, up_hbm, kv_hbm, byte_gain, pool_query, patch_gain, live_bias, starts,
    enc_hbm, mixed_hbm,
    q, k, v, q_next, o_send, o_recv, s_send, s_recv, o_own, s_own, enc, w, pooled, lifted, patch_in,
    x_q, x_kv, kv_all, q_all, o_out, o_in,
    load_sem, out_sem, q_ss, q_rs, o_ss, o_rs, s_ss, s_rs, wy_ss, wy_rs, wz_ss, wz_rs,
    wp_ss, wp_rs, wm_ss, wm_rs, w2_ss, w2_rs, wc_ss, wc_rs,
    kz_ss, kz_rs, qz_ss, qz_rs, yp_ss, yp_rs, ym_ss, ym_rs, yf_ss, yf_rs, oz_ss, oz_rs,
):
    s = lax.axis_index("seq")
    d = lax.axis_index("doc")
    z, yh = lax.div(s, 4), lax.rem(s, 4)
    x, rest, core = lax.div(d, 4), lax.rem(d, 4), lax.rem(d, 2)
    after, before = lax.rem(s + 1, 32), lax.rem(s + 31, 32)

    def along_y(step):
        return z * 4 + lax.rem(yh + step, 4)

    def along_z(step):
        return lax.rem(z + step, 8) * 4 + yh

    x_up, x_down = lax.rem(x + 1, 4) * 4 + rest, lax.rem(x + 3, 4) * 4 + rest
    partner = d + 1 - 2 * core

    def remote(src, dst, send, recv, seq, doc):
        return pltpu.make_async_remote_copy(
            src_ref=src, dst_ref=dst, send_sem=send, recv_sem=recv,
            device_id={"seq": seq, "doc": doc}, device_id_type=MESH,
        )

    def load(hbm, dst, which, h):
        cols = pl.ds(pl.multiple_of(h * 128, 128), 128)
        return pltpu.make_async_copy(hbm.at[:, cols], dst.at[h], load_sem.at[which, h])

    part = 2 * x + core

    def own_weights():
        ours = w.at[part, s]
        first = pl.multiple_of(part * 256, 256)
        return [
            pltpu.make_async_copy(up_hbm.at[:, pl.ds(first, 128)], ours.at[0:32], load_sem.at[3, 0]),
            pltpu.make_async_copy(up_hbm.at[:, pl.ds(first + 128, 128)], ours.at[32:64], load_sem.at[3, 1]),
            pltpu.make_async_copy(
                kv_hbm.at[:, pl.ds(pl.multiple_of(part * 128, 128), 128)], ours.at[64:128], load_sem.at[3, 2]
            ),
        ]

    @pl.loop(0, 8)
    def _(h):
        load(q_hbm, q, 0, h).start()

    for copy in own_weights():
        copy.start()

    @pl.loop(0, 8)
    def _(h):
        load(k_hbm, k, 1, h).start()
        load(v_hbm, v, 2, h).start()

    barrier = pltpu.get_barrier_semaphore()
    peers = [(after, d), (before, d), (s, x_up), (s, x_down), (s, partner)]
    peers += [(along_y(i), d) for i in (1, 2, 3)] + [(along_z(i), d) for i in NEAR_FIRST]
    for seq, doc in peers:
        pl.semaphore_signal(barrier, inc=1, device_id={"seq": seq, "doc": doc}, device_id_type=MESH)
    pl.semaphore_wait(barrier, len(peers))

    def send_query(h):
        return remote(q.at[h], q_next.at[h], q_ss.at[h], q_rs.at[h], before, d)

    @pl.loop(0, 8)
    def _(h):
        load(q_hbm, q, 0, h).wait()
        send_query(h).start()

    def block(p, step):
        return w.at[p, pl.ds(lax.rem(z + step, 8) * 4, 4)]

    def part_of(step):
        return 2 * lax.rem(x + step, 4) + core

    def w_y(step):
        ours = w.at[part, s]
        return remote(ours, ours, wy_ss.at[step - 1], wy_rs.at[step - 1], along_y(step), d)

    def w_y_arrival(step):
        slot = w.at[part, along_y(4 - step)]
        return remote(slot, slot, wy_ss.at[step - 1], wy_rs.at[step - 1], along_y(step), d)

    def w_z(step):
        ours = block(part, 0)
        return remote(ours, ours, wz_ss.at[step - 1], wz_rs.at[step - 1], along_z(step), d)

    def w_z_arrival(step):
        slot = block(part, 8 - step)
        return remote(slot, slot, wz_ss.at[step - 1], wz_rs.at[step - 1], along_z(step), d)

    def w_up(p, i):
        slot = block(p, i)
        return remote(slot, slot, wp_ss.at[i], wp_rs.at[i], s, x_up)

    def w_down(p, i):
        slot = block(p, i)
        return remote(slot, slot, wm_ss.at[i], wm_rs.at[i], s, x_down)

    def w_far(p, i):
        slot = block(p, i)
        return remote(slot, slot, w2_ss.at[i], w2_rs.at[i], s, x_up if i % 2 == 0 else x_down)

    def w_core(step, i, mine=True):
        p = part_of(step) if mine else 2 * lax.rem(x + step, 4) + 1 - core
        slot = block(p, i)
        return remote(slot, slot, wc_ss.at[step, i], wc_rs.at[step, i], s, partner)

    def spread(i):
        w_up(part, i).start()
        w_down(part, i).start()
        w_core(0, i).start()

    def from_x(i):
        w_up(part_of(3), i).wait_recv()
        if i % 2 == 0:
            w_far(part_of(3), i).start()
        w_core(3, i).start()
        w_down(part_of(1), i).wait_recv()
        if i % 2 == 1:
            w_far(part_of(1), i).start()
        w_core(1, i).start()

    def from_far(i):
        w_far(part_of(2), i).wait_recv()
        w_core(2, i).start()

    def weights_y():
        for copy in own_weights():
            copy.wait()
        for i in (1, 2, 3):
            w_y(i).start()

    def weights_z():
        for i in (1, 2, 3):
            w_y_arrival(i).wait_recv()
        for i in NEAR_FIRST:
            w_z(i).start()
        spread(0)

    def from_z(i):
        w_z_arrival(i).wait_recv()
        spread(8 - i)

    weights_y()

    def local_head(h):
        load(k_hbm, k, 1, h).wait()
        load(v_hbm, v, 2, h).wait()
        for half in (0, 1):
            rows, keys = pl.ds(256 * half, 256), 256 * (half + 1)
            t = dot_t(q[h, rows, :], k[h, 0:keys, :]) * BYTE_SCALE
            t = jnp.where(iota((256, keys), 1) <= iota((256, keys), 0) + 256 * half, t, NEG)
            peak = jnp.max(t, axis=1, keepdims=True)
            e = jnp.exp2(t - peak)
            total = jnp.sum(e, axis=1, keepdims=True)
            o_own[h, rows, :] = dot(e.astype(BF16), v[h, 0:keys, :]) * (1.0 / total)
            s_own[h, :, rows] = as_row(peak + jnp.log(total) * LOG2E)

    def remote_head(h):
        send_query(h).wait_recv()
        for half in (0, 1):
            rows, keys = pl.ds(256 * half, 256), 512 - 256 * half
            t = dot_t(q_next[h, rows, :], k[h, 256 * half : 512, :]) * BYTE_SCALE
            t = jnp.where(iota((256, keys), 1) > iota((256, keys), 0), t, NEG)
            peak = jnp.max(t, axis=1, keepdims=True)
            e = jnp.exp2(t - peak)
            total = jnp.sum(e, axis=1, keepdims=True)
            o = dot(e.astype(BF16), v[h, 256 * half : 512, :]) * (1.0 / total)
            o_send[h, rows, :] = o.astype(BF16)
            lse = peak + jnp.log(total) * LOG2E
            if half == 1:
                lse = jnp.where(iota((256, 1), 0) == 255, NEG, lse)
            s_send[h, :, rows] = as_row(lse)

    def send_out(h):
        return remote(o_send.at[h], o_recv.at[h], o_ss.at[h], o_rs.at[h], after, d)

    def send_stat(h):
        return remote(s_send.at[h], s_recv.at[h], s_ss.at[h], s_rs.at[h], after, d)

    @pl.loop(0, 8)
    def _(h):
        local_head(h)

        @pl.when(h == 1)
        def _():
            weights_z()

    stages = {
        0: [(from_z, 1), (from_z, 7)],
        1: [(from_z, 2), (from_z, 6), (from_x, 0)],
        2: [(from_z, 3), (from_z, 5), (from_x, 7), (from_x, 1), (from_far, 0)],
        3: [(from_z, 4), (from_x, 6), (from_x, 2), (from_far, 7), (from_far, 1)],
        4: [(from_x, 5), (from_x, 3), (from_far, 6), (from_far, 2)],
        5: [(from_x, 4), (from_far, 5), (from_far, 3)],
        6: [(from_far, 4)],
    }

    def forward(stage):
        for step, i in stage:
            step(i)

    @pl.loop(0, 8)
    def _(h):
        remote_head(h)
        send_out(h).start()
        send_stat(h).start()
        for at, stage in stages.items():
            pl.when(h == at)(functools.partial(forward, stage))

    def merge(h, squares):
        send_out(h).wait_recv()
        send_stat(h).wait_recv()
        own = s_own[h]
        other = jnp.where(s == 0, NEG, s_recv[h])
        peak = jnp.maximum(own, other)
        a, b = jnp.exp2(own - peak), jnp.exp2(other - peak)
        share = jnp.transpose(jnp.broadcast_to(b / (a + b), (128, 512)))
        mine = o_own[h]
        mix = mine + share * (o_recv[h].astype(F32) - mine)
        o_own[h] = mix
        return squares + mix * mix

    squares = lax.fori_loop(0, 8, merge, jnp.zeros((512, 128), F32))
    scale = lax.rsqrt(jnp.sum(squares, axis=1, keepdims=True) * (1.0 / 1024) + EPS)
    for h in range(8):
        enc[h] = (o_own[h] * scale * byte_gain[h : h + 1, :]).astype(BF16)
    enc_out = pltpu.make_async_copy(enc, enc_hbm, out_sem.at[0])
    enc_out.start()

    row = jnp.broadcast_to(starts[...].astype(F32), (80, 80))
    r80, c80 = iota((80, 80), 0), iota((80, 80), 1)
    first = jnp.sum(jnp.where(c80 == r80, row, 0.0), axis=1, keepdims=True)
    stop = jnp.sum(jnp.where(c80 == r80 + 1, row, 0.0), axis=1, keepdims=True)
    stop = jnp.where(iota((80, 1), 0) == 79, 512.0, stop)
    at = iota((80, 512), 1).astype(F32)
    member = (at >= first) & (at < stop)
    for h in range(8):
        score = dot_t(pool_query[...], enc[h])[h : h + 1, :] * BYTE_SCALE
        t = jnp.where(member, score, NEG)
        peak = jnp.max(t, axis=1, keepdims=True)
        e = jnp.where(member, jnp.exp2(t - peak), 0.0)
        total = jnp.sum(e, axis=1, keepdims=True)
        weights = (e / jnp.where(total > 0.0, total, 1.0)).astype(BF16)
        pooled[:, 128 * h : 128 * h + 128] = dot(weights, enc[h]).astype(BF16)

    for step in (0, 3, 1, 2):
        for i in (0, 7, 1, 6, 2, 5, 3, 4):
            w_core(step, i, mine=False).wait_recv()

    def lift(p, squares):
        left = w[p, :, 0:32, :].reshape(1024, 128)
        right = w[p, :, 32:64, :].reshape(1024, 128)
        got = dot(pooled[...], jnp.concatenate([left, right], axis=1))
        lifted[p] = got
        return squares + got * got

    squares = lax.fori_loop(0, 8, lift, jnp.zeros((80, 256), F32))
    scale = lax.rsqrt(jnp.sum(squares, axis=1, keepdims=True) * (1.0 / 2048) + EPS)
    for p in range(8):
        got = (lifted[p] * scale * patch_gain[p : p + 1, :]).astype(BF16)
        x_q[p] = got
        patch_in[:, 256 * p : 256 * p + 256] = got
    low = iota((80, 128), 1) < 64

    @pl.loop(0, 4)
    def _(p):
        keys = w[p, :, 64:128, :].reshape(2048, 128)
        values = w[p + 4, :, 64:128, :].reshape(2048, 128)
        got = dot(patch_in[...], jnp.concatenate([keys, values], axis=1))
        key, value = got[:, 0:128], got[:, 128:256]
        x_kv[2 * p] = jnp.where(low, key, pltpu.roll(value, 64, 1)).astype(BF16)
        x_kv[2 * p + 1] = jnp.where(low, pltpu.roll(key, 64, 1), value).astype(BF16)

    def kv_to(i):
        to = lax.rem(z + i, 8)
        return remote(x_kv.at[to], kv_all.at[z, yh], kz_ss.at[i - 1], kz_rs.at[i - 1], along_z(i), d)

    def q_to(i):
        to = lax.rem(z + i, 8)
        return remote(x_q.at[to], q_all.at[z], qz_ss.at[i - 1], qz_rs.at[i - 1], along_z(i), d)

    def kv_from(slot):
        i = lax.rem(z - slot + 7, 8)
        dst = kv_all.at[slot, yh]
        return remote(dst, dst, kz_ss.at[i], kz_rs.at[i], s, partner)

    def q_from(slot):
        i = lax.rem(z - slot + 7, 8)
        dst = q_all.at[slot]
        return remote(dst, dst, qz_ss.at[i], qz_rs.at[i], s, partner)

    for i in NEAR_FIRST:
        kv_to(i).start()
    for i in NEAR_FIRST:
        q_to(i).start()
    kv_all[z, yh] = x_kv[z]
    q_all[z] = x_q[z]

    y_up, y_down = lax.rem(yh + 1, 4), lax.rem(yh + 3, 4)

    def kv_up(slot, whose):
        ours = kv_all.at[slot, whose]
        return remote(ours, ours, yp_ss.at[slot], yp_rs.at[slot], along_y(1), d)

    def kv_down(slot, whose):
        ours = kv_all.at[slot, whose]
        return remote(ours, ours, ym_ss.at[slot], ym_rs.at[slot], along_y(3), d)

    def kv_far_up(slot, whose):
        ours = kv_all.at[slot, whose]
        return remote(ours, ours, yf_ss.at[slot], yf_rs.at[slot], along_y(1), d)

    def kv_far_down(slot, whose):
        ours = kv_all.at[slot, whose]
        return remote(ours, ours, yf_ss.at[slot], yf_rs.at[slot], along_y(3), d)

    @pl.loop(0, 8)
    def _(slot):
        @pl.when(slot != z)
        def _():
            kv_from(slot).wait_recv()

        kv_up(slot, yh).start()
        kv_down(slot, yh).start()

    def relay(slot):
        kv_up(slot, y_down).wait_recv()
        kv_down(slot, y_up).wait_recv()

        @pl.when(lax.rem(slot, 2) == 0)
        def _():
            kv_far_up(slot, y_down).start()

        @pl.when(lax.rem(slot, 2) == 1)
        def _():
            kv_far_down(slot, y_up).start()

    def out_to(to):
        return remote(o_out.at[to], o_in.at[z], oz_ss.at[to], oz_rs.at[z], to * 4 + yh, d)

    def out_from(slot):
        dst = o_in.at[slot]
        return remote(dst, dst, oz_ss.at[slot], oz_rs.at[slot], s, partner)

    r320 = iota((320, 1), 0)
    r320 = jnp.where(r320 >= 240, r320 - 240, jnp.where(r320 >= 160, r320 - 160, jnp.where(r320 >= 80, r320 - 80, r320)))

    def patch_block(slot):
        @pl.when(slot != z)
        def _():
            q_from(slot).wait_recv()

        heads = []
        for tile in (0, 1):
            pair = q_all[slot, :, 128 * tile : 128 * tile + 128].astype(F32)
            heads += [jnp.where(low, pair, 0.0), jnp.where(low, pltpu.roll(pair, 64, 1), 0.0)]
        query = jnp.concatenate(heads, axis=0).astype(BF16)
        query_pos = slot * 320 + yh * 80 + r320

        def chunk(c, state):
            peak, total, acc = state
            rows = kv_all[pl.ds(2 * c, 2)].reshape(640, 128)
            t = dot_t(query, rows) * PATCH_SCALE + live_bias[c]
            t = jnp.where(c * 640 + iota((320, 640), 1) <= query_pos, t, NEG)
            peak_new = jnp.maximum(peak, jnp.max(t, axis=1, keepdims=True))
            e = jnp.exp2(t - peak_new)
            fade = jnp.exp2(peak - peak_new)
            total = total * fade + jnp.sum(e, axis=1, keepdims=True)
            acc = acc * fade + dot(e.astype(BF16), rows)
            return peak_new, total, acc

        start = (jnp.full((320, 1), NEG, F32), jnp.zeros((320, 1), F32), jnp.zeros((320, 128), F32))
        _, total, acc = lax.fori_loop(0, lax.div(slot, 2) + 1, chunk, start)
        out = acc * (1.0 / total)
        for tile in (0, 1):
            even, odd = out[160 * tile : 160 * tile + 80], out[160 * tile + 80 : 160 * tile + 160]
            o_out[slot, :, 128 * tile : 128 * tile + 128] = jnp.where(low, pltpu.roll(even, 64, 1), odd).astype(BF16)

        @pl.when(slot != z)
        def _():
            out_to(slot).start()

        @pl.when(slot == z)
        def _():
            o_in[slot] = o_out[slot]

    def far_arrival(slot):
        kv_far_up(slot, lax.rem(yh + 2, 4)).wait_recv()

    for slot in (0, 1):
        relay(slot)
    far_arrival(0)

    @pl.loop(0, 8)
    def _(slot):
        @pl.when(slot < 6)
        def _():
            relay(slot + 2)

        @pl.when(slot < 7)
        def _():
            far_arrival(slot + 1)

        patch_block(slot)

    @pl.loop(0, 8)
    def _(slot):
        @pl.when(slot != z)
        def _():
            out_from(slot).wait_recv()

    mixed_out = pltpu.make_async_copy(o_in, mixed_hbm, out_sem.at[1])
    mixed_out.start()

    @pl.loop(0, 8)
    def _(h):
        send_query(h).wait_send()
        send_out(h).wait_send()
        send_stat(h).wait_send()
        kv_up(h, yh).wait_send()
        kv_down(h, yh).wait_send()
        kv_far_up(h, yh).wait_send()

        @pl.when(h != z)
        def _():
            out_to(h).wait_send()

    for i in (1, 2, 3):
        w_y(i).wait_send()
    for i in NEAR_FIRST:
        w_z(i).wait_send()
        kv_to(i).wait_send()
        q_to(i).wait_send()
    for i in range(8):
        w_up(part, i).wait_send()
        w_down(part, i).wait_send()
        w_far(part, i).wait_send()
        for step in range(4):
            w_core(step, i).wait_send()
    enc_out.wait()
    mixed_out.wait()


def decode_kernel(enc, mixed, out_gain, dec_gain, starts, byte_out, patch_out, cross):
    row = starts[...]
    wide = jnp.broadcast_to(row.astype(F32), (80, 80))
    first = jnp.sum(jnp.where(iota((80, 80), 1) == iota((80, 80), 0), wide, 0.0), axis=1, keepdims=True)
    alive = (first < 512.0).astype(F32)
    squares = jnp.zeros((80, 256), F32)
    for h in range(8):
        got = mixed[h].astype(F32)
        squares = squares + got * got
    scale = lax.rsqrt(jnp.sum(squares, axis=1, keepdims=True) * (1.0 / 2048) + EPS)
    allowed = row <= iota((512, 80), 0)
    squares = jnp.zeros((512, 128), F32)
    for h in range(8):
        patch = (mixed[h].astype(F32) * scale * out_gain[h : h + 1, :] * alive).astype(BF16)
        patch_out[:, 256 * h : 256 * h + 256] = patch
        t = jnp.where(allowed, dot_t(enc[h], patch[:, 0:128]) * BYTE_SCALE, NEG)
        peak = jnp.max(t, axis=1, keepdims=True)
        e = jnp.exp2(t - peak)
        total = jnp.sum(e, axis=1, keepdims=True)
        got = dot(e.astype(BF16), patch[:, 128:256]) * (1.0 / total)
        cross[h] = got
        squares = squares + got * got
    scale = lax.rsqrt(jnp.sum(squares, axis=1, keepdims=True) * (1.0 / 1024) + EPS)
    for h in range(8):
        byte_out[:, 128 * h : 128 * h + 128] = (cross[h] * scale * dec_gain[h : h + 1, :]).astype(BF16)


def per_device(
    byte_q, byte_k, byte_v, byte_gain, pool_query, w_up, patch_gain, w_kv, out_gain, dec_gain, patch_start
):
    starts = lax.dynamic_slice_in_dim(patch_start, lax.axis_index("seq"), 1, 0)
    live_bias = jnp.where(patch_start < 512, 0.0, NEG).astype(F32).reshape(4, 1, 640)
    hbm = pl.BlockSpec(memory_space=pl.ANY)
    vmem = pl.BlockSpec(memory_space=pltpu.VMEM)
    dma = pltpu.SemaphoreType.DMA
    enc, mixed = pl.pallas_call(
        main_kernel,
        out_shape=(
            jax.ShapeDtypeStruct((8, 512, 128), BF16),
            jax.ShapeDtypeStruct((8, 80, 256), BF16),
        ),
        in_specs=[hbm] * 5 + [vmem] * 5,
        out_specs=(hbm, hbm),
        scratch_shapes=[
            pltpu.VMEM((8, 512, 128), BF16),
            pltpu.VMEM((8, 512, 128), BF16),
            pltpu.VMEM((8, 512, 128), BF16),
            pltpu.VMEM((8, 512, 128), BF16),
            pltpu.VMEM((8, 512, 128), BF16),
            pltpu.VMEM((8, 512, 128), BF16),
            pltpu.VMEM((8, 1, 512), F32),
            pltpu.VMEM((8, 1, 512), F32),
            pltpu.VMEM((8, 512, 128), F32),
            pltpu.VMEM((8, 1, 512), F32),
            pltpu.VMEM((8, 512, 128), BF16),
            pltpu.VMEM((8, 32, 128, 128), BF16),
            pltpu.VMEM((80, 1024), BF16),
            pltpu.VMEM((8, 80, 256), F32),
            pltpu.VMEM((80, 2048), BF16),
            pltpu.VMEM((8, 80, 256), BF16),
            pltpu.VMEM((8, 80, 128), BF16),
            pltpu.VMEM((8, 4, 80, 128), BF16),
            pltpu.VMEM((8, 80, 256), BF16),
            pltpu.VMEM((8, 80, 256), BF16),
            pltpu.VMEM((8, 80, 256), BF16),
            dma((4, 8)),
            dma((2,)),
            *[dma((8,))] * 6,
            *[dma((3,))] * 2,
            *[dma((7,))] * 2,
            *[dma((8,))] * 6,
            *[dma((4, 8))] * 2,
            *[dma((7,))] * 4,
            *[dma((8,))] * 8,
        ],
        compiler_params=pltpu.CompilerParams(
            collective_id=0, has_side_effects=True, vmem_limit_bytes=60 * 1024 * 1024
        ),
    )(
        byte_q, byte_k, byte_v, w_up, w_kv,
        byte_gain.astype(F32).reshape(8, 128),
        jnp.concatenate([pool_query, pool_query], axis=0),
        patch_gain.astype(F32).reshape(8, 256),
        live_bias, starts,
    )
    return pl.pallas_call(
        decode_kernel,
        out_shape=(
            jax.ShapeDtypeStruct((512, 1024), BF16),
            jax.ShapeDtypeStruct((80, 2048), BF16),
        ),
        in_specs=[vmem] * 5,
        out_specs=(vmem, vmem),
        scratch_shapes=[pltpu.VMEM((8, 512, 128), F32)],
        compiler_params=pltpu.CompilerParams(vmem_limit_bytes=40 * 1024 * 1024),
    )(
        enc, mixed, out_gain.astype(F32).reshape(8, 256), dec_gain.astype(F32).reshape(8, 128), starts
    )


def solution(mesh):
    placed = (
        P(("doc", "seq"), None),
        P(("doc", "seq"), None),
        P(("doc", "seq"), None),
        P(),
        P(),
        P("seq", None),
        P(),
        P("seq", None),
        P(),
        P(),
        P("doc", None),
    )
    return jax.shard_map(
        per_device,
        mesh=mesh,
        in_specs=placed,
        out_specs=(P(("doc", "seq"), None), P(("doc", "seq"), None)),
        check_vma=False,
    )
```

time: 407 us -> 182 us (0.45)
  the two profiles are of different devices: /device:TPU:10 before, /device:TPU:24 now
where the time goes in v1:
time: 182 us
  Pallas kernels  175 us (96%)
  local copies, waits for them, and re-layouts  5.55 us (3%)
    pallas_call x1, Pallas kernels, per_device(): pl.pallas_call(main_kernel, out_shape=(jax.ShapeDtypeStruct((8, 512, 128)...  172 us

profile of v1, /device:TPU:24, one launch (start us, length us, event | category | flops | bytes accessed | tf_op | source)
XLA Modules:
  0.0 182.0 jit_solution(1758978352096356602)
XLA Ops:
  0.6 0.0 copy-start.6
  0.6 1.2 constant_dynamic-slice_fusion.starts
  1.9 0.0 copy-done.6
  1.9 0.0 copy-start.7
  1.9 0.0 copy-start.8
  1.9 0.6 bitcast_convert_fusion.1.byte_gain
  2.5 0.1 copy-done.7
  2.6 0.0 copy-start.4
  2.6 0.0 copy-start.5
  2.6 0.6 pad_maximum_fusion.pool_query
  3.2 0.0 copy-done.8
  3.2 0.0 copy-start.3
  3.2 0.1 copy-done.4
  3.3 0.6 reshape.39.patch_gain
  3.9 0.0 copy-done.5
  3.9 0.0 copy-done.3
  3.9 0.7 reshape.31.live_bias
  4.6 171.6 %shard_map.122 = (bf16[8,512,128]{2,1,0:T(8,128)(2,1)}, bf16[8,80,256]{2,1,0:T(8,128)(2,1)}) custom-call(bf16[512,1024]{1,0:T(8,128)(2,1)} %q_hbm.1, bf16[512,1024]{1,0:T(8,128)(2,1)} %k_hbm.1, bf16[512,1024]{1,0:T(8,128)(2,1)} %v_hbm.1, bf16[32,2048]{1,0:T(8,128)(2,1)} %up_hbm.1, bf16[64,1024]{1,0:T(8,128)(2,1)} %kv_hbm.1, ...), custom_call_target="tpu_custom_call" | custom-call | tf_op jit(solution)/shard_map/pallas_call | solution.py:522
  176.2 0.0 copy-start.2
  176.2 0.6 copy-done.2
  176.9 0.0 copy-start
  176.9 1.2 copy-done
  178.1 0.0 copy-start.1
  178.1 1.0 copy-done.1
  179.1 2.9 %shard_map.123 = (bf16[512,1024]{1,0:T(8,128)(2,1)}, bf16[80,2048]{1,0:T(8,128)(2,1)}) custom-call(bf16[8,512,128]{2,1,0:T(8,128)(2,1)S(1)} %copy-done, bf16[8,80,256]{2,1,0:T(8,128)(2,1)S(1)} %copy-done.1, f32[8,256]{1,0:T(8,128)S(1)} %reshape.41.out_gain, f32[8,128]{1,0:T(8,128)S(1)} %bitcast_convert_fusion.dec_gain, s32[1,80]{1,0:T(1,128)S(1)} %copy-done.2), custom_call_target="tpu_custom_call" | custom-call | tf_op jit(solution)/shard_map/pallas_call | solution.py:572
  (3 shorter events, 0.0 us)
Async XLA Ops:
  0.6 1.2 copy-start.6
  1.9 0.7 copy-start.7
  1.9 1.3 copy-start.8
  2.6 0.7 copy-start.4
  2.6 1.3 copy-start.5
  3.2 0.7 copy-start.3
  176.2 0.6 copy-start.2
  176.9 1.2 copy-start
  178.1 1.0 copy-start.1

commit v2 on v1

v2 whole, which is shorter than its diff:
```python
import functools

import jax
import jax.numpy as jnp
from jax import lax
from jax.experimental import pallas as pl
from jax.experimental.pallas import tpu as pltpu
from jax.sharding import PartitionSpec as P

EPS = 1e-06
LOG2E = 1.4426950408889634
BYTE_SCALE = 128 ** (-0.5) * LOG2E
PATCH_SCALE = 64 ** (-0.5) * LOG2E
NEG = -1e30
F32 = jnp.float32
BF16 = jnp.bfloat16
MESH = pl.DeviceIdType.MESH
IN_FLIGHT = 5
NEAR_FIRST = (1, 7, 2, 6, 3, 5, 4)


def dot(a, b):
    return lax.dot_general(a, b, (((1,), (0,)), ((), ())), preferred_element_type=F32)


def dot_t(a, b):
    return lax.dot_general(a, b, (((1,), (1,)), ((), ())), preferred_element_type=F32)


def iota(shape, dim):
    return lax.broadcasted_iota(jnp.int32, shape, dim)


def gain_row(ref, i, width):
    return ref[pl.ds(i * width, width)].astype(F32).reshape(1, width)


def as_row(column):
    return jnp.transpose(jnp.broadcast_to(column, (column.shape[0], 128)))[0:1]


def main_kernel(
    q_hbm, k_hbm, v_hbm, up_hbm, kv_hbm, byte_gain, pool_query, patch_gain, starts,
    enc_hbm, mixed_hbm,
    q, k, v, q_next, o_send, o_recv, s_send, s_recv, o_own, s_own, enc, w, pooled, lifted, patch_in,
    x_q, x_kv, kv_all, q_all, o_out, o_in, live_bias,
    load_sem, out_sem, q_ss, q_rs, o_ss, o_rs, s_ss, s_rs, wy_ss, wy_rs, zu_ss, zu_rs, zd_ss, zd_rs,
    wp_ss, wp_rs, wm_ss, wm_rs, w2_ss, w2_rs, wc_ss, wc_rs,
    kz_ss, kz_rs, qz_ss, qz_rs, yp_ss, yp_rs, ym_ss, ym_rs, yf_ss, yf_rs, oz_ss, oz_rs,
):
    s = lax.axis_index("seq")
    d = lax.axis_index("doc")
    z, yh = lax.div(s, 4), lax.rem(s, 4)
    x, rest, core = lax.div(d, 4), lax.rem(d, 4), lax.rem(d, 2)
    after, before = lax.rem(s + 1, 32), lax.rem(s + 31, 32)

    def along_y(step):
        return z * 4 + lax.rem(yh + step, 4)

    def along_z(step):
        return lax.rem(z + step, 8) * 4 + yh

    x_up, x_down = lax.rem(x + 1, 4) * 4 + rest, lax.rem(x + 3, 4) * 4 + rest
    partner = d + 1 - 2 * core

    def remote(src, dst, send, recv, seq, doc):
        return pltpu.make_async_remote_copy(
            src_ref=src, dst_ref=dst, send_sem=send, recv_sem=recv,
            device_id={"seq": seq, "doc": doc}, device_id_type=MESH,
        )

    def load(hbm, dst, which, h):
        cols = pl.ds(pl.multiple_of(h * 128, 128), 128)
        return pltpu.make_async_copy(hbm.at[:, cols], dst.at[h], load_sem.at[which])

    def loaded(dst, which):
        pltpu.make_async_copy(dst, dst, load_sem.at[which]).wait()

    def sent(ref, sem):
        remote(ref, ref, sem.at[0], sem.at[0], s, partner).wait_send()

    part = 2 * x + core

    def own_weights():
        ours = w.at[part, s]
        first = pl.multiple_of(part * 256, 256)
        return [
            pltpu.make_async_copy(up_hbm.at[:, pl.ds(first, 128)], ours.at[0:32], load_sem.at[3]),
            pltpu.make_async_copy(up_hbm.at[:, pl.ds(first + 128, 128)], ours.at[32:64], load_sem.at[3]),
            pltpu.make_async_copy(
                kv_hbm.at[:, pl.ds(pl.multiple_of(part * 128, 128), 128)], ours.at[64:128], load_sem.at[3]
            ),
        ]

    for copy in own_weights():
        copy.start()

    @pl.loop(0, 8)
    def _(h):
        load(q_hbm, q, 0, h).start()

    @pl.loop(0, 8)
    def _(h):
        load(k_hbm, k, 1, h).start()
        load(v_hbm, v, 2, h).start()

    barrier = pltpu.get_barrier_semaphore()
    peers = [(after, d), (before, d), (s, x_up), (s, x_down), (s, partner)]
    peers += [(along_y(i), d) for i in (1, 2, 3)] + [(along_z(i), d) for i in NEAR_FIRST]
    for seq, doc in peers:
        pl.semaphore_signal(barrier, inc=1, device_id={"seq": seq, "doc": doc}, device_id_type=MESH)
    pl.semaphore_wait(barrier, len(peers))

    def block(p, step):
        return w.at[p, pl.ds(lax.rem(z + step, 8) * 4, 4)]

    def part_of(step):
        return 2 * lax.rem(x + step, 4) + core

    def w_y(step):
        ours = w.at[part, s]
        return remote(ours, ours, wy_ss.at[0], wy_rs.at[0], along_y(step), d)

    def z_up(step):
        slot = block(part, (9 - step) % 8)
        return remote(slot, slot, zu_ss.at[0], zu_rs.at[step - 1], along_z(1), d)

    def z_down(step):
        slot = block(part, step - 1)
        return remote(slot, slot, zd_ss.at[0], zd_rs.at[step - 1], along_z(7), d)

    def w_up(p, i):
        slot = block(p, i)
        return remote(slot, slot, wp_ss.at[0], wp_rs.at[i], s, x_up)

    def w_down(p, i):
        slot = block(p, i)
        return remote(slot, slot, wm_ss.at[0], wm_rs.at[i], s, x_down)

    def w_far(p, i):
        slot = block(p, i)
        return remote(slot, slot, w2_ss.at[0], w2_rs.at[i], s, x_up if i % 2 == 0 else x_down)

    def w_core(step, i):
        slot = block(part_of(step), i)
        return remote(slot, slot, wc_ss.at[0], wc_rs.at[0], s, partner)

    def spread(i):
        w_up(part, i).start()
        w_down(part, i).start()
        w_core(0, i).start()

    def from_x(i):
        w_up(part_of(3), i).wait_recv()
        if i % 2 == 0:
            w_far(part_of(3), i).start()
        w_core(3, i).start()
        w_down(part_of(1), i).wait_recv()
        if i % 2 == 1:
            w_far(part_of(1), i).start()
        w_core(1, i).start()

    def from_far(i):
        w_far(part_of(2), i).wait_recv()
        w_core(2, i).start()

    def weights_y():
        loaded(w.at[part, s], 3)
        for i in (1, 2, 3):
            w_y(i).start()

    def weights_z():
        three = w.at[part, pl.ds(z * 4, 3)]
        remote(three, three, wy_ss.at[0], wy_rs.at[0], s, partner).wait_recv()
        z_up(1).start()
        z_down(1).start()
        spread(0)

    def from_z(step):
        z_up(step).wait_recv()
        if step < 4:
            z_up(step + 1).start()
            z_down(step).wait_recv()
        if step < 3:
            z_down(step + 1).start()
        spread(8 - step)
        if step < 4:
            spread(step)

    weights_y()

    def send_query(unit):
        h, half = lax.div(unit, 2), lax.rem(unit, 2)
        rows = pl.ds(pl.multiple_of(half * 256, 256), 256)
        return remote(q.at[h, rows], q_next.at[h, rows], q_ss.at[0], q_rs.at[unit], before, d)

    loaded(q, 0)
    for unit in range(IN_FLIGHT):
        send_query(unit).start()

    def local_head(h):
        for half in (0, 1):
            rows, keys = pl.ds(256 * half, 256), 256 * (half + 1)
            t = dot_t(q[h, rows, :], k[h, 0:keys, :]) * BYTE_SCALE
            t = jnp.where(iota((256, keys), 1) <= iota((256, keys), 0) + 256 * half, t, NEG)
            peak = jnp.max(t, axis=1, keepdims=True)
            e = jnp.exp2(t - peak)
            total = jnp.sum(e, axis=1, keepdims=True)
            o_own[h, rows, :] = dot(e.astype(BF16), v[h, 0:keys, :]) * (1.0 / total)
            s_own[h, :, rows] = as_row(peak + jnp.log(total) * LOG2E)

    def remote_half(h, half):
        rows, keys = pl.ds(256 * half, 256), 512 - 256 * half
        t = dot_t(q_next[h, rows, :], k[h, 256 * half : 512, :]) * BYTE_SCALE
        t = jnp.where(iota((256, keys), 1) > iota((256, keys), 0), t, NEG)
        peak = jnp.max(t, axis=1, keepdims=True)
        e = jnp.exp2(t - peak)
        total = jnp.sum(e, axis=1, keepdims=True)
        o = dot(e.astype(BF16), v[h, 256 * half : 512, :]) * (1.0 / total)
        o_send[h, rows, :] = o.astype(BF16)
        lse = peak + jnp.log(total) * LOG2E
        if half == 1:
            lse = jnp.where(iota((256, 1), 0) == 255, NEG, lse)
        s_send[h, :, rows] = as_row(lse)

    def send_out(h, half):
        rows = pl.ds(256 * half, 256)
        return remote(o_send.at[h, rows], o_recv.at[h, rows], o_ss.at[0], o_rs.at[h], after, d)

    def whole_out(h):
        return remote(o_send.at[h], o_recv.at[h], o_ss.at[0], o_rs.at[h], after, d)

    def send_stat(h):
        return remote(s_send.at[h], s_recv.at[h], s_ss.at[0], s_rs.at[h], after, d)

    local_stages = {4: [(weights_z,)]}
    stages = {
        0: [(from_z, 1)],
        2: [(from_z, 2)],
        4: [(from_z, 3), (from_x, 0)],
        6: [(from_z, 4), (from_x, 7)],
        7: [(from_x, 1)],
        8: [(from_x, 6), (from_far, 0)],
        10: [(from_x, 2), (from_far, 7)],
        11: [(from_x, 5), (from_far, 1)],
        12: [(from_x, 3), (from_far, 6)],
        13: [(from_x, 4), (from_far, 2)],
        14: [(from_far, 5)],
        15: [(from_far, 3), (from_far, 4)],
    }

    def forward(stage):
        for step, *i in stage:
            step(*i)

    loaded(k, 1)
    loaded(v, 2)

    @pl.loop(0, 8)
    def _(h):
        local_head(h)
        for at, stage in local_stages.items():
            pl.when(h == at)(functools.partial(forward, stage))

    p80, n80 = iota((80, 640), 0), iota((80, 640), 1)
    repeat = n80 == p80
    for i in range(1, 8):
        repeat = repeat | (n80 == p80 + 80 * i)
    of_row = iota((8, 640), 1) - 80 * iota((8, 640), 0)
    of_row = (of_row >= 0) & (of_row < 80)
    for c in range(4):
        live = (starts[8 * c : 8 * c + 8, :] < 512).astype(BF16)
        spread_out = dot(live, repeat.astype(BF16))
        live_bias[c] = jnp.sum(jnp.where(of_row, (spread_out - 1.0) * -NEG, 0.0), axis=0, keepdims=True)

    @pl.loop(0, 8)
    def _(h):
        for half in (0, 1):
            unit = 2 * h + half
            send_query(unit).wait_recv()

            @pl.when(unit < 16 - IN_FLIGHT)
            def _():
                send_query(unit + IN_FLIGHT).start()

            remote_half(h, half)
            send_out(h, half).start()
            if half == 1:
                send_stat(h).start()
            for at, stage in stages.items():
                if at % 2 == half:
                    pl.when(h == at // 2)(functools.partial(forward, stage))

    def merge(h, squares):
        whole_out(h).wait_recv()
        send_stat(h).wait_recv()
        own = s_own[h]
        other = jnp.where(s == 0, NEG, s_recv[h])
        peak = jnp.maximum(own, other)
        a, b = jnp.exp2(own - peak), jnp.exp2(other - peak)
        share = jnp.transpose(jnp.broadcast_to(b / (a + b), (128, 512)))
        mine = o_own[h]
        mix = mine + share * (o_recv[h].astype(F32) - mine)
        o_own[h] = mix
        return squares + mix * mix

    squares = lax.fori_loop(0, 8, merge, jnp.zeros((512, 128), F32))
    scale = lax.rsqrt(jnp.sum(squares, axis=1, keepdims=True) * (1.0 / 1024) + EPS)
    for h in range(8):
        enc[h] = (o_own[h] * scale * gain_row(byte_gain, h, 128)).astype(BF16)
    enc_out = pltpu.make_async_copy(enc, enc_hbm, out_sem.at[0])
    enc_out.start()

    row = jnp.broadcast_to(starts[pl.ds(s, 1), :].astype(F32), (80, 80))
    r80, c80 = iota((80, 80), 0), iota((80, 80), 1)
    first = jnp.sum(jnp.where(c80 == r80, row, 0.0), axis=1, keepdims=True)
    stop = jnp.sum(jnp.where(c80 == r80 + 1, row, 0.0), axis=1, keepdims=True)
    stop = jnp.where(iota((80, 1), 0) == 79, 512.0, stop)
    at = iota((80, 512), 1).astype(F32)
    member = (at >= first) & (at < stop)
    for h in range(8):
        score = dot_t(pool_query[...], enc[h])[h : h + 1, :] * BYTE_SCALE
        t = jnp.where(member, score, NEG)
        peak = jnp.max(t, axis=1, keepdims=True)
        e = jnp.where(member, jnp.exp2(t - peak), 0.0)
        total = jnp.sum(e, axis=1, keepdims=True)
        weights = (e / jnp.where(total > 0.0, total, 1.0)).astype(BF16)
        pooled[:, 128 * h : 128 * h + 128] = dot(weights, enc[h]).astype(BF16)

    half_of_w = w.at[0:4]
    remote(half_of_w, half_of_w, wc_ss.at[0], wc_rs.at[0], s, partner).wait_recv()

    def lift(p, squares):
        left = w[p, :, 0:32, :].reshape(1024, 128)
        right = w[p, :, 32:64, :].reshape(1024, 128)
        got = dot(pooled[...], jnp.concatenate([left, right], axis=1))
        lifted[p] = got
        return squares + got * got

    squares = lax.fori_loop(0, 8, lift, jnp.zeros((80, 256), F32))
    scale = lax.rsqrt(jnp.sum(squares, axis=1, keepdims=True) * (1.0 / 2048) + EPS)
    for p in range(8):
        got = (lifted[p] * scale * gain_row(patch_gain, p, 256)).astype(BF16)
        x_q[p] = got
        patch_in[:, 256 * p : 256 * p + 256] = got
    low = iota((80, 128), 1) < 64

    @pl.loop(0, 4)
    def _(p):
        keys = w[p, :, 64:128, :].reshape(2048, 128)
        values = w[p + 4, :, 64:128, :].reshape(2048, 128)
        got = dot(patch_in[...], jnp.concatenate([keys, values], axis=1))
        key, value = got[:, 0:128], got[:, 128:256]
        x_kv[2 * p] = jnp.where(low, key, pltpu.roll(value, 64, 1)).astype(BF16)
        x_kv[2 * p + 1] = jnp.where(low, pltpu.roll(key, 64, 1), value).astype(BF16)

    def kv_to(i):
        to = lax.rem(z + i, 8)
        return remote(x_kv.at[to], kv_all.at[z, yh], kz_ss.at[0], kz_rs.at[i - 1], along_z(i), d)

    def q_to(i):
        to = lax.rem(z + i, 8)
        return remote(x_q.at[to], q_all.at[z], qz_ss.at[0], qz_rs.at[i - 1], along_z(i), d)

    def kv_from(slot):
        i = lax.rem(z - slot + 7, 8)
        dst = kv_all.at[slot, yh]
        return remote(dst, dst, kz_ss.at[0], kz_rs.at[i], s, partner)

    def q_from(slot):
        i = lax.rem(z - slot + 7, 8)
        dst = q_all.at[slot]
        return remote(dst, dst, qz_ss.at[0], qz_rs.at[i], s, partner)

    for i in NEAR_FIRST:
        kv_to(i).start()
    for i in NEAR_FIRST:
        q_to(i).start()
    kv_all[z, yh] = x_kv[z]
    q_all[z] = x_q[z]

    sent(q, q_ss)
    sent(o_send, o_ss)
    sent(s_send, s_ss)
    sent(w.at[0, 0:3], wy_ss)
    sent(w.at[0, 0:16], zu_ss)
    sent(w.at[0, 0:12], zd_ss)
    sent(w.at[0], wp_ss)
    sent(w.at[0], wm_ss)
    sent(w.at[0], w2_ss)
    sent(half_of_w, wc_ss)

    y_up, y_down = lax.rem(yh + 1, 4), lax.rem(yh + 3, 4)

    def kv_up(slot, whose):
        ours = kv_all.at[slot, whose]
        return remote(ours, ours, yp_ss.at[0], yp_rs.at[slot], along_y(1), d)

    def kv_down(slot, whose):
        ours = kv_all.at[slot, whose]
        return remote(ours, ours, ym_ss.at[0], ym_rs.at[slot], along_y(3), d)

    def kv_far_up(slot, whose):
        ours = kv_all.at[slot, whose]
        return remote(ours, ours, yf_ss.at[0], yf_rs.at[slot], along_y(1), d)

    def kv_far_down(slot, whose):
        ours = kv_all.at[slot, whose]
        return remote(ours, ours, yf_ss.at[0], yf_rs.at[slot], along_y(3), d)

    def forward_kv(slot):
        @pl.when(slot != z)
        def _():
            kv_from(slot).wait_recv()

        kv_up(slot, yh).start()
        kv_down(slot, yh).start()

    def relay(slot):
        kv_up(slot, y_down).wait_recv()
        kv_down(slot, y_up).wait_recv()

        @pl.when(lax.rem(slot, 2) == 0)
        def _():
            kv_far_up(slot, y_down).start()

        @pl.when(lax.rem(slot, 2) == 1)
        def _():
            kv_far_down(slot, y_up).start()

    def out_to(to):
        return remote(o_out.at[to], o_in.at[z], oz_ss.at[0], oz_rs.at[z], to * 4 + yh, d)

    def out_from(slot):
        dst = o_in.at[slot]
        return remote(dst, dst, oz_ss.at[0], oz_rs.at[slot], s, partner)

    r320 = iota((320, 1), 0)
    r320 = jnp.where(r320 >= 240, r320 - 240, jnp.where(r320 >= 160, r320 - 160, jnp.where(r320 >= 80, r320 - 80, r320)))

    low_keys = iota((640, 128), 1) < 64

    def gathered_query(slot):
        @pl.when(slot != z)
        def _():
            q_from(slot).wait_recv()

        heads = []
        for tile in (0, 1):
            pair = q_all[slot, :, 128 * tile : 128 * tile + 128].astype(F32)
            heads += [jnp.where(low, pair, 0.0), jnp.where(low, pltpu.roll(pair, 64, 1), 0.0)]
        return jnp.concatenate(heads, axis=0).astype(BF16)

    def patch_pair(pair):
        slots = (2 * pair, 2 * pair + 1)
        queries = [gathered_query(slot) for slot in slots]

        def chunk(c, state, last):
            rows = kv_all[pl.ds(2 * c, 2)].reshape(640, 128)
            values = jnp.where(low_keys, jnp.ones((), BF16), rows)
            bias = live_bias[c]
            new = []
            for i in (0, 1):
                peak, acc = state[i]
                t = dot_t(queries[i], rows) * PATCH_SCALE + bias
                if last:
                    t = jnp.where(iota((320, 640), 1) <= i * 320 + yh * 80 + r320, t, NEG)
                peak_new = jnp.maximum(peak, jnp.max(t, axis=1, keepdims=True))
                e = jnp.exp2(t - peak_new).astype(BF16)
                new.append((peak_new, acc * jnp.exp2(peak - peak_new) + dot(e, values)))
            return tuple(new)

        start = (jnp.full((320, 1), NEG, F32), jnp.zeros((320, 128), F32))
        state = lax.fori_loop(0, pair, functools.partial(chunk, last=False), (start, start))
        state = chunk(pair, state, True)
        for slot, (_, acc) in zip(slots, state):
            out = acc * (1.0 / acc[:, 0:1])
            for tile in (0, 1):
                even, odd = out[160 * tile : 160 * tile + 80], out[160 * tile + 80 : 160 * tile + 160]
                o_out[slot, :, 128 * tile : 128 * tile + 128] = jnp.where(low, pltpu.roll(even, 64, 1), odd).astype(BF16)

            @pl.when(slot != z)
            def _():
                out_to(slot).start()

            @pl.when(slot == z)
            def _():
                o_in[slot] = o_out[slot]

    def far_arrival(slot):
        kv_far_up(slot, lax.rem(yh + 2, 4)).wait_recv()

    @pl.loop(0, 4)
    def _(slot):
        forward_kv(slot)

    @pl.loop(0, 4)
    def _(pair):
        @pl.when(pair == 0)
        def _():
            relay(0)
            relay(1)
            forward_kv(4)
            forward_kv(5)

        @pl.when(pair == 1)
        def _():
            forward_kv(6)
            forward_kv(7)

        @pl.when(pair < 3)
        def _():
            relay(2 * pair + 2)
            relay(2 * pair + 3)

        far_arrival(2 * pair)
        far_arrival(2 * pair + 1)
        patch_pair(pair)

    def mixed_out(slot):
        return pltpu.make_async_copy(o_in.at[slot], mixed_hbm.at[slot], out_sem.at[1])

    @pl.loop(0, 8)
    def _(slot):
        @pl.when(slot != z)
        def _():
            out_from(slot).wait_recv()

        mixed_out(slot).start()

    sent(x_kv.at[0:7], kz_ss)
    sent(x_q.at[0:7], qz_ss)
    sent(x_kv, yp_ss)
    sent(x_kv, ym_ss)
    sent(x_kv, yf_ss)
    sent(o_out.at[0:7], oz_ss)
    enc_out.wait()
    pltpu.make_async_copy(o_in, mixed_hbm, out_sem.at[1]).wait()


def decode_kernel(enc_hbm, mixed_hbm, out_gain, dec_gain, starts, byte_out, patch_out, cross, enc, mixed, sem, enc_sem):
    mixed_in = pltpu.make_async_copy(mixed_hbm, mixed, sem)
    mixed_in.start()

    enc_in = pltpu.make_async_copy(enc_hbm, enc, enc_sem)
    enc_in.start()
    row = starts[pl.ds(lax.axis_index("seq"), 1), :]
    wide = jnp.broadcast_to(row.astype(F32), (80, 80))
    first = jnp.sum(jnp.where(iota((80, 80), 1) == iota((80, 80), 0), wide, 0.0), axis=1, keepdims=True)
    alive = (first < 512.0).astype(F32)
    mixed_in.wait()
    enc_in.wait()
    squares = jnp.zeros((80, 256), F32)
    for h in range(8):
        got = mixed[h].astype(F32)
        squares = squares + got * got
    scale = lax.rsqrt(jnp.sum(squares, axis=1, keepdims=True) * (1.0 / 2048) + EPS)
    allowed = row <= iota((512, 80), 0)
    squares = jnp.zeros((512, 128), F32)
    for h in range(8):
        patch = (mixed[h].astype(F32) * scale * gain_row(out_gain, h, 256) * alive).astype(BF16)
        patch_out[:, 256 * h : 256 * h + 256] = patch
        t = jnp.where(allowed, dot_t(enc[h], patch[:, 0:128]) * BYTE_SCALE, NEG)
        peak = jnp.max(t, axis=1, keepdims=True)
        e = jnp.exp2(t - peak)
        total = jnp.sum(e, axis=1, keepdims=True)
        got = dot(e.astype(BF16), patch[:, 128:256]) * (1.0 / total)
        cross[h] = got
        squares = squares + got * got
    scale = lax.rsqrt(jnp.sum(squares, axis=1, keepdims=True) * (1.0 / 1024) + EPS)
    for h in range(8):
        byte_out[:, 128 * h : 128 * h + 128] = (cross[h] * scale * gain_row(dec_gain, h, 128)).astype(BF16)


def per_device(
    byte_q, byte_k, byte_v, byte_gain, pool_query, w_up, patch_gain, w_kv, out_gain, dec_gain, patch_start
):
    hbm = pl.BlockSpec(memory_space=pl.ANY)
    vmem = pl.BlockSpec(memory_space=pltpu.VMEM)
    dma = pltpu.SemaphoreType.DMA
    enc, mixed = pl.pallas_call(
        main_kernel,
        out_shape=(
            jax.ShapeDtypeStruct((8, 512, 128), BF16),
            jax.ShapeDtypeStruct((8, 80, 256), BF16),
        ),
        in_specs=[hbm] * 5 + [vmem] * 4,
        out_specs=(hbm, hbm),
        scratch_shapes=[
            pltpu.VMEM((8, 512, 128), BF16),
            pltpu.VMEM((8, 512, 128), BF16),
            pltpu.VMEM((8, 512, 128), BF16),
            pltpu.VMEM((8, 512, 128), BF16),
            pltpu.VMEM((8, 512, 128), BF16),
            pltpu.VMEM((8, 512, 128), BF16),
            pltpu.VMEM((8, 1, 512), F32),
            pltpu.VMEM((8, 1, 512), F32),
            pltpu.VMEM((8, 512, 128), F32),
            pltpu.VMEM((8, 1, 512), F32),
            pltpu.VMEM((8, 512, 128), BF16),
            pltpu.VMEM((8, 32, 128, 128), BF16),
            pltpu.VMEM((80, 1024), BF16),
            pltpu.VMEM((8, 80, 256), F32),
            pltpu.VMEM((80, 2048), BF16),
            pltpu.VMEM((8, 80, 256), BF16),
            pltpu.VMEM((8, 80, 128), BF16),
            pltpu.VMEM((8, 4, 80, 128), BF16),
            pltpu.VMEM((8, 80, 256), BF16),
            pltpu.VMEM((8, 80, 256), BF16),
            pltpu.VMEM((8, 80, 256), BF16),
            pltpu.VMEM((4, 1, 640), F32),
            dma((4,)),
            dma((2,)),
            *[dma((1,)), dma((16,))],
            *[dma((1,)), dma((8,))] * 2,
            *[dma((1,)), dma((1,))],
            *[dma((1,)), dma((4,))],
            *[dma((1,)), dma((3,))],
            *[dma((1,)), dma((8,))] * 3,
            *[dma((1,)), dma((1,))],
            *[dma((1,)), dma((7,))] * 2,
            *[dma((1,)), dma((8,))] * 4,
        ],
        compiler_params=pltpu.CompilerParams(
            collective_id=0, has_side_effects=True, vmem_limit_bytes=60 * 1024 * 1024
        ),
    )(
        byte_q, byte_k, byte_v, w_up, w_kv,
        byte_gain, pool_query, patch_gain, patch_start,
    )
    return pl.pallas_call(
        decode_kernel,
        out_shape=(
            jax.ShapeDtypeStruct((512, 1024), BF16),
            jax.ShapeDtypeStruct((80, 2048), BF16),
        ),
        in_specs=[hbm] * 2 + [vmem] * 3,
        out_specs=(vmem, vmem),
        scratch_shapes=[
            pltpu.VMEM((8, 512, 128), F32),
            pltpu.VMEM((8, 512, 128), BF16),
            pltpu.VMEM((8, 80, 256), BF16),
            dma,
            dma,
        ],
        compiler_params=pltpu.CompilerParams(vmem_limit_bytes=60 * 1024 * 1024),
    )(
        enc, mixed, out_gain, dec_gain, patch_start
    )


def solution(mesh):
    placed = (
        P(("doc", "seq"), None),
        P(("doc", "seq"), None),
        P(("doc", "seq"), None),
        P(),
        P(),
        P("seq", None),
        P(),
        P("seq", None),
        P(),
        P(),
        P("doc", None),
    )
    return jax.shard_map(
        per_device,
        mesh=mesh,
        in_specs=placed,
        out_specs=(P(("doc", "seq"), None), P(("doc", "seq"), None)),
        check_vma=False,
    )
```

time: 182 us -> 127 us (0.70)
  the two profiles are of different devices: /device:TPU:24 before, /device:TPU:8 now
where the time goes in v2:
time: 127 us
  Pallas kernels  126 us (99%)
    pallas_call x1, Pallas kernels, per_device(): pl.pallas_call(main_kernel, out_shape=(jax.ShapeDtypeStruct((8, 512, 128)...  121 us
    pallas_call x1, Pallas kernels, per_device(): pl.pallas_call(decode_kernel, out_shape=(jax.ShapeDtypeStruct((512, 1024)...  4.97 us

profile of v2, /device:TPU:8, one launch (start us, length us, event | category | flops | bytes accessed | tf_op | source)
XLA Modules:
  0.0 126.5 jit_solution(4178853912027271025)
XLA Ops:
  0.6 120.9 %shard_map.122 = (bf16[8,512,128]{2,1,0:T(8,128)(2,1)}, bf16[8,80,256]{2,1,0:T(8,128)(2,1)}) custom-call(bf16[512,1024]{1,0:T(8,128)(2,1)} %q_hbm.1, bf16[512,1024]{1,0:T(8,128)(2,1)} %k_hbm.1, bf16[512,1024]{1,0:T(8,128)(2,1)} %v_hbm.1, bf16[32,2048]{1,0:T(8,128)(2,1)} %up_hbm.1, bf16[64,1024]{1,0:T(8,128)(2,1)} %kv_hbm.1, bf16[1024]{0:T(1024)(128)(2,1)} %byte_gain.1, ...), custom_call_target="tpu_custom_call" | custom-call | tf_op jit(solution)/shard_map/pallas_call | solution.py:581
  121.6 5.0 %shard_map.123 = (bf16[512,1024]{1,0:T(8,128)(2,1)}, bf16[80,2048]{1,0:T(8,128)(2,1)}) custom-call(bf16[8,512,128]{2,1,0:T(8,128)(2,1)} %get-tuple-element.4.enc_hbm, bf16[8,80,256]{2,1,0:T(8,128)(2,1)} %get-tuple-element.5.mixed_hbm, bf16[2048]{0:T(1024)(128)(2,1)} %out_gain.1, bf16[1024]{0:T(1024)(128)(2,1)} %dec_gain.1, s32[32,80]{1,0:T(8,128)} %starts.3), custom_call_target="tpu_custom_call" | custom-call | tf_op jit(solution)/shard_map/pallas_call | solution.py:631

commit v3 on v2

--- a/solution.py
+++ b/solution.py
@@ -15,8 +15,8 @@
 F32 = jnp.float32
 BF16 = jnp.bfloat16
 MESH = pl.DeviceIdType.MESH
-IN_FLIGHT = 5
-NEAR_FIRST = (1, 7, 2, 6, 3, 5, 4)
+IN_FLIGHT = 4
+FAR_FIRST = (4, 3, 5, 2, 6, 1, 7)
 
 
 def dot(a, b):
@@ -42,9 +42,9 @@
 def main_kernel(
     q_hbm, k_hbm, v_hbm, up_hbm, kv_hbm, byte_gain, pool_query, patch_gain, starts,
     enc_hbm, mixed_hbm,
-    q, k, v, q_next, o_send, o_recv, s_send, s_recv, o_own, s_own, enc, w, pooled, lifted, patch_in,
+    q, k, v, q_next, k_prev, v_prev, o_send, o_recv, s_send, s_recv, o_own, s_own, enc, w, pooled, lifted, patch_in,
     x_q, x_kv, kv_all, q_all, o_out, o_in, live_bias,
-    load_sem, out_sem, q_ss, q_rs, o_ss, o_rs, s_ss, s_rs, wy_ss, wy_rs, zu_ss, zu_rs, zd_ss, zd_rs,
+    load_sem, out_sem, kp_ss, kp_rs, q_ss, q_rs, o_ss, o_rs, s_ss, s_rs, wy_ss, wy_rs, zu_ss, zu_rs, zd_ss, zd_rs,
     wp_ss, wp_rs, wm_ss, wm_rs, w2_ss, w2_rs, wc_ss, wc_rs,
     kz_ss, kz_rs, qz_ss, qz_rs, yp_ss, yp_rs, ym_ss, ym_rs, yf_ss, yf_rs, oz_ss, oz_rs,
 ):
@@ -106,7 +106,7 @@
 
     barrier = pltpu.get_barrier_semaphore()
     peers = [(after, d), (before, d), (s, x_up), (s, x_down), (s, partner)]
-    peers += [(along_y(i), d) for i in (1, 2, 3)] + [(along_z(i), d) for i in NEAR_FIRST]
+    peers += [(along_y(i), d) for i in (1, 2, 3)] + [(along_z(i), d) for i in FAR_FIRST]
     for seq, doc in peers:
         pl.semaphore_signal(barrier, inc=1, device_id={"seq": seq, "doc": doc}, device_id_type=MESH)
     pl.semaphore_wait(barrier, len(peers))
@@ -194,9 +194,16 @@
         rows = pl.ds(pl.multiple_of(half * 256, 256), 256)
         return remote(q.at[h, rows], q_next.at[h, rows], q_ss.at[0], q_rs.at[unit], before, d)
 
+    def send_keys(which):
+        own, dst = ((k, k_prev), (v, v_prev))[which]
+        return remote(own.at[7], dst, kp_ss.at[which], kp_rs.at[which], after, d)
+
     loaded(q, 0)
-    for unit in range(IN_FLIGHT):
-        send_query(unit).start()
+    send_query(0).start()
+    loaded(k, 1)
+    loaded(v, 2)
+    send_keys(0).start()
+    send_keys(1).start()
 
     def local_head(h):
         for half in (0, 1):
@@ -209,19 +216,28 @@
             o_own[h, rows, :] = dot(e.astype(BF16), v[h, 0:keys, :]) * (1.0 / total)
             s_own[h, :, rows] = as_row(peak + jnp.log(total) * LOG2E)
 
-    def remote_half(h, half):
-        rows, keys = pl.ds(256 * half, 256), 512 - 256 * half
-        t = dot_t(q_next[h, rows, :], k[h, 256 * half : 512, :]) * BYTE_SCALE
-        t = jnp.where(iota((256, keys), 1) > iota((256, keys), 0), t, NEG)
+    def cross_half(half, queries, keys, values, o_dst, s_dst):
+        rows, n = pl.ds(256 * half, 256), 512 - 256 * half
+        t = dot_t(queries[rows, :], keys[256 * half : 512, :]) * BYTE_SCALE
+        t = jnp.where(iota((256, n), 1) > iota((256, n), 0), t, NEG)
         peak = jnp.max(t, axis=1, keepdims=True)
         e = jnp.exp2(t - peak)
         total = jnp.sum(e, axis=1, keepdims=True)
-        o = dot(e.astype(BF16), v[h, 256 * half : 512, :]) * (1.0 / total)
-        o_send[h, rows, :] = o.astype(BF16)
+        o = dot(e.astype(BF16), values[256 * half : 512, :]) * (1.0 / total)
+        o_dst[rows, :] = o.astype(BF16)
         lse = peak + jnp.log(total) * LOG2E
         if half == 1:
             lse = jnp.where(iota((256, 1), 0) == 255, NEG, lse)
-        s_send[h, :, rows] = as_row(lse)
+        s_dst[:, rows] = as_row(lse)
+
+    def remote_half(h, half):
+        cross_half(half, q_next.at[h], k.at[h], v.at[h], o_send.at[h], s_send.at[h])
+
+    def last_head():
+        send_keys(0).wait_recv()
+        send_keys(1).wait_recv()
+        for half in (0, 1):
+            cross_half(half, q.at[7], k_prev, v_prev, o_recv.at[7], s_recv.at[7])
 
     def send_out(h, half):
         rows = pl.ds(256 * half, 256)
@@ -233,34 +249,35 @@
     def send_stat(h):
         return remote(s_send.at[h], s_recv.at[h], s_ss.at[0], s_rs.at[h], after, d)
 
-    local_stages = {4: [(weights_z,)]}
     stages = {
         0: [(from_z, 1)],
+        1: [(from_x, 0)],
         2: [(from_z, 2)],
-        4: [(from_z, 3), (from_x, 0)],
-        6: [(from_z, 4), (from_x, 7)],
-        7: [(from_x, 1)],
-        8: [(from_x, 6), (from_far, 0)],
-        10: [(from_x, 2), (from_far, 7)],
-        11: [(from_x, 5), (from_far, 1)],
-        12: [(from_x, 3), (from_far, 6)],
-        13: [(from_x, 4), (from_far, 2)],
-        14: [(from_far, 5)],
-        15: [(from_far, 3), (from_far, 4)],
+        4: [(from_z, 3), (from_x, 7)],
+        5: [(from_x, 1)],
+        6: [(from_z, 4), (from_far, 0)],
+        7: [(from_x, 6), (last_head,)],
+        8: [(from_x, 2)],
+        9: [(from_far, 7)],
+        10: [(from_x, 5), (from_far, 1)],
+        11: [(from_x, 3), (from_x, 4)],
+        12: [(from_far, 6)],
+        13: [(from_far, 2)],
     }
 
     def forward(stage):
         for step, *i in stage:
             step(*i)
 
-    loaded(k, 1)
-    loaded(v, 2)
-
-    @pl.loop(0, 8)
+    @pl.loop(0, 4)
     def _(h):
         local_head(h)
-        for at, stage in local_stages.items():
-            pl.when(h == at)(functools.partial(forward, stage))
+
+        @pl.when(h < 3)
+        def _():
+            send_query(h + 1).start()
+
+    weights_z()
 
     p80, n80 = iota((80, 640), 0), iota((80, 640), 1)
     repeat = n80 == p80
@@ -273,13 +290,13 @@
         spread_out = dot(live, repeat.astype(BF16))
         live_bias[c] = jnp.sum(jnp.where(of_row, (spread_out - 1.0) * -NEG, 0.0), axis=0, keepdims=True)
 
-    @pl.loop(0, 8)
+    @pl.loop(0, 7)
     def _(h):
         for half in (0, 1):
             unit = 2 * h + half
             send_query(unit).wait_recv()
 
-            @pl.when(unit < 16 - IN_FLIGHT)
+            @pl.when(unit < 14 - IN_FLIGHT)
             def _():
                 send_query(unit + IN_FLIGHT).start()
 
@@ -287,13 +304,24 @@
             send_out(h, half).start()
             if half == 1:
                 send_stat(h).start()
+
+            @pl.when(h < 2)
+            def _():
+                local_head(4 + unit)
+
             for at, stage in stages.items():
                 if at % 2 == half:
                     pl.when(h == at // 2)(functools.partial(forward, stage))
 
+    for i in (5, 3, 4):
+        from_far(i)
+
     def merge(h, squares):
-        whole_out(h).wait_recv()
-        send_stat(h).wait_recv()
+        @pl.when(h < 7)
+        def _():
+            whole_out(h).wait_recv()
+            send_stat(h).wait_recv()
+
         own = s_own[h]
         other = jnp.where(s == 0, NEG, s_recv[h])
         peak = jnp.maximum(own, other)
@@ -372,16 +400,18 @@
         dst = q_all.at[slot]
         return remote(dst, dst, qz_ss.at[0], qz_rs.at[i], s, partner)
 
-    for i in NEAR_FIRST:
+    for i in FAR_FIRST:
         kv_to(i).start()
-    for i in NEAR_FIRST:
+    for i in FAR_FIRST:
         q_to(i).start()
     kv_all[z, yh] = x_kv[z]
     q_all[z] = x_q[z]
 
-    sent(q, q_ss)
-    sent(o_send, o_ss)
-    sent(s_send, s_ss)
+    sent(q.at[0:7], q_ss)
+    sent(o_send.at[0:7], o_ss)
+    sent(s_send.at[0:7], s_ss)
+    send_keys(0).wait_send()
+    send_keys(1).wait_send()
     sent(w.at[0, 0:3], wy_ss)
     sent(w.at[0, 0:16], zu_ss)
     sent(w.at[0, 0:12], zd_ss)
@@ -591,6 +621,8 @@
             pltpu.VMEM((8, 512, 128), BF16),
             pltpu.VMEM((8, 512, 128), BF16),
             pltpu.VMEM((8, 512, 128), BF16),
+            pltpu.VMEM((512, 128), BF16),
+            pltpu.VMEM((512, 128), BF16),
             pltpu.VMEM((8, 512, 128), BF16),
             pltpu.VMEM((8, 512, 128), BF16),
             pltpu.VMEM((8, 1, 512), F32),
@@ -610,6 +642,8 @@
             pltpu.VMEM((8, 80, 256), BF16),
             pltpu.VMEM((4, 1, 640), F32),
             dma((4,)),
+            dma((2,)),
+            dma((2,)),
             dma((2,)),
             *[dma((1,)), dma((16,))],
             *[dma((1,)), dma((8,))] * 2,

time: 127 us -> 118 us (0.929)
  the two profiles are of different devices: /device:TPU:8 before, /device:TPU:64 now
where the time goes in v3:
time: 118 us
  Pallas kernels  117 us (99%)
    pallas_call x1, Pallas kernels, per_device(): pl.pallas_call(main_kernel, out_shape=(jax.ShapeDtypeStruct((8, 512, 128)...  112 us
    pallas_call x1, Pallas kernels, per_device(): pl.pallas_call(decode_kernel, out_shape=(jax.ShapeDtypeStruct((512, 1024)...  4.97 us

profile of v3, /device:TPU:64, one launch (start us, length us, event | category | flops | bytes accessed | tf_op | source)
XLA Modules:
  0.0 118.0 jit_solution(9018640886169900805)
XLA Ops:
  0.6 112.4 %shard_map.122 = (bf16[8,512,128]{2,1,0:T(8,128)(2,1)}, bf16[8,80,256]{2,1,0:T(8,128)(2,1)}) custom-call(bf16[512,1024]{1,0:T(8,128)(2,1)} %q_hbm.1, bf16[512,1024]{1,0:T(8,128)(2,1)} %k_hbm.1, bf16[512,1024]{1,0:T(8,128)(2,1)} %v_hbm.1, bf16[32,2048]{1,0:T(8,128)(2,1)} %up_hbm.1, bf16[64,1024]{1,0:T(8,128)(2,1)} %kv_hbm.1, bf16[1024]{0:T(1024)(128)(2,1)} %byte_gain.1, ...), custom_call_target="tpu_custom_call" | custom-call | tf_op jit(solution)/shard_map/pallas_call | solution.py:611
  113.0 5.0 %shard_map.123 = (bf16[512,1024]{1,0:T(8,128)(2,1)}, bf16[80,2048]{1,0:T(8,128)(2,1)}) custom-call(bf16[8,512,128]{2,1,0:T(8,128)(2,1)} %get-tuple-element.4.enc_hbm, bf16[8,80,256]{2,1,0:T(8,128)(2,1)} %get-tuple-element.5.mixed_hbm, bf16[2048]{0:T(1024)(128)(2,1)} %out_gain.1, bf16[1024]{0:T(1024)(128)(2,1)} %dec_gain.1, s32[32,80]{1,0:T(8,128)} %starts.3), custom_call_target="tpu_custom_call" | custom-call | tf_op jit(solution)/shard_map/pallas_call | solution.py:665

commit v4 on v3

--- a/solution.py
+++ b/solution.py
@@ -350,9 +350,9 @@
         score = dot_t(pool_query[...], enc[h])[h : h + 1, :] * BYTE_SCALE
         t = jnp.where(member, score, NEG)
         peak = jnp.max(t, axis=1, keepdims=True)
-        e = jnp.where(member, jnp.exp2(t - peak), 0.0)
+        e = jnp.exp2(t - peak)
         total = jnp.sum(e, axis=1, keepdims=True)
-        weights = (e / jnp.where(total > 0.0, total, 1.0)).astype(BF16)
+        weights = (e * jnp.where(first < 512.0, 1.0 / total, 0.0)).astype(BF16)
         pooled[:, 128 * h : 128 * h + 128] = dot(weights, enc[h]).astype(BF16)
 
     half_of_w = w.at[0:4]
@@ -402,8 +402,12 @@
 
     for i in FAR_FIRST:
         kv_to(i).start()
-    for i in FAR_FIRST:
-        q_to(i).start()
+
+    def send_queries():
+        for i in FAR_FIRST:
+            q_to(i).start()
+
+    pl.when(z < 4)(send_queries)
     kv_all[z, yh] = x_kv[z]
     q_all[z] = x_q[z]
 
@@ -524,6 +528,8 @@
     def _(slot):
         forward_kv(slot)
 
+    pl.when(z >= 4)(send_queries)
+
     @pl.loop(0, 4)
     def _(pair):
         @pl.when(pair == 0)
@@ -568,12 +574,23 @@
     pltpu.make_async_copy(o_in, mixed_hbm, out_sem.at[1]).wait()
 
 
-def decode_kernel(enc_hbm, mixed_hbm, out_gain, dec_gain, starts, byte_out, patch_out, cross, enc, mixed, sem, enc_sem):
+def decode_kernel(
+    enc_hbm, mixed_hbm, out_gain_hbm, dec_gain_hbm, starts_hbm, byte_out, patch_out,
+    cross, enc, mixed, out_gain, dec_gain, starts, sem, enc_sem, small_sem,
+):
+    small = [
+        pltpu.make_async_copy(src, dst, small_sem.at[i])
+        for i, (src, dst) in enumerate(((out_gain_hbm, out_gain), (dec_gain_hbm, dec_gain), (starts_hbm, starts)))
+    ]
     mixed_in = pltpu.make_async_copy(mixed_hbm, mixed, sem)
     mixed_in.start()
 
+    for copy in small:
+        copy.start()
     enc_in = pltpu.make_async_copy(enc_hbm, enc, enc_sem)
     enc_in.start()
+    for copy in small:
+        copy.wait()
     row = starts[pl.ds(lax.axis_index("seq"), 1), :]
     wide = jnp.broadcast_to(row.astype(F32), (80, 80))
     first = jnp.sum(jnp.where(iota((80, 80), 1) == iota((80, 80), 0), wide, 0.0), axis=1, keepdims=True)
@@ -668,14 +685,18 @@
             jax.ShapeDtypeStruct((512, 1024), BF16),
             jax.ShapeDtypeStruct((80, 2048), BF16),
         ),
-        in_specs=[hbm] * 2 + [vmem] * 3,
+        in_specs=[hbm] * 5,
         out_specs=(vmem, vmem),
         scratch_shapes=[
             pltpu.VMEM((8, 512, 128), F32),
             pltpu.VMEM((8, 512, 128), BF16),
             pltpu.VMEM((8, 80, 256), BF16),
+            pltpu.VMEM((2048,), BF16),
+            pltpu.VMEM((1024,), BF16),
+            pltpu.VMEM((32, 80), jnp.int32),
             dma,
             dma,
+            dma((3,)),
         ],
         compiler_params=pltpu.CompilerParams(vmem_limit_bytes=60 * 1024 * 1024),
     )(

time: 118 us -> 117 us (level)
  the two profiles are of different devices: /device:TPU:64 before, /device:TPU:2 now
where the time goes in v4:
time: 117 us
  Pallas kernels  116 us (99%)
    pallas_call x1, Pallas kernels, per_device(): pl.pallas_call(main_kernel, out_shape=(jax.ShapeDtypeStruct((8, 512, 128)...  112 us
    pallas_call x1, Pallas kernels, per_device(): pl.pallas_call(decode_kernel, out_shape=(jax.ShapeDtypeStruct((512, 1024)...  4.29 us

profile of v4, /device:TPU:2, one launch (start us, length us, event | category | flops | bytes accessed | tf_op | source)
XLA Modules:
  0.0 116.6 jit_solution(6873619187744962085)
XLA Ops:
  0.6 111.7 %shard_map.122 = (bf16[8,512,128]{2,1,0:T(8,128)(2,1)}, bf16[8,80,256]{2,1,0:T(8,128)(2,1)}) custom-call(bf16[512,1024]{1,0:T(8,128)(2,1)} %q_hbm.1, bf16[512,1024]{1,0:T(8,128)(2,1)} %k_hbm.1, bf16[512,1024]{1,0:T(8,128)(2,1)} %v_hbm.1, bf16[32,2048]{1,0:T(8,128)(2,1)} %up_hbm.1, bf16[64,1024]{1,0:T(8,128)(2,1)} %kv_hbm.1, bf16[1024]{0:T(1024)(128)(2,1)} %byte_gain.1, ...), custom_call_target="tpu_custom_call" | custom-call | tf_op jit(solution)/shard_map/pallas_call | solution.py:628
  112.3 4.3 %shard_map.123 = (bf16[512,1024]{1,0:T(8,128)(2,1)}, bf16[80,2048]{1,0:T(8,128)(2,1)}) custom-call(bf16[8,512,128]{2,1,0:T(8,128)(2,1)} %get-tuple-element.4.enc_hbm, bf16[8,80,256]{2,1,0:T(8,128)(2,1)} %get-tuple-element.5.mixed_hbm, bf16[2048]{0:T(1024)(128)(2,1)} %out_gain_hbm.1, bf16[1024]{0:T(1024)(128)(2,1)} %dec_gain_hbm.1, s32[32,80]{1,0:T(8,128)} %starts_hbm.1), custom_call_target="tpu_custom_call" | custom-call | tf_op jit(solution)/shard_map/pallas_call | solution.py:682
